TPU v7x, 512 devices: a whole 4x8x8 slice. The times are simulated.
512 devices in a mesh: wide: 128 (over y, z, core), narrow: 4 (over x).
Axes of the slice: x: 4, y: 8, z: 8, core: 2. Of those that a mesh axis runs over, the one named last changes fastest.
Arguments:
- queries: bfloat16 [65536, 2048], P(('wide', 'narrow')), may hold values from -8 to 8
- key_tensor: bfloat16 [65536, 256], P(('wide', 'narrow')), may hold values from -8 to 8
- value_tensor: bfloat16 [65536, 256], P(('wide', 'narrow')), may hold values from -8 to 8
- decay_logarithm: float32 [2, 65536], P(None, ('wide', 'narrow')), may hold values from -2 to 0
- lin_gain: float32 [2048], replicated, may hold values from 0.25 to 1.75
- routes: int32 [65536, 2], P(('wide', 'narrow')), may hold values from 0 to 31, all different within a row; in each aligned block of 128 rows (0 to 127, 128 to 255, ...) at most 12 rows name the same one
- route_weight: float32 [65536, 2], P(('wide', 'narrow')), may hold values from 0.2 to 1
- w_up: bfloat16 [2048, 45056], P(None, 'wide'), may hold values from -0.125 to 0.125
- w_down: bfloat16 [45056, 2048], P('wide'), may hold values from -0.15625 to 0.15625
Outputs:
- layer_out: bfloat16 [65536, 2048], P(('wide', 'narrow'))
Inputs may be any that keep to these rules, and one draw needn't show every extreme that they name: `routes`: each row names 2 different experts. In each aligned block of 128 rows no expert is named more than 12 times, and in some block some expert is named exactly 12 times.
All inputs are finite; a program needn't handle non-finite values.
Results may differ from a plain program's by a relative error of at most 0.0055.
Values may be sent and summed in bfloat16 or wider, within the bound.
No kernel may reach another device: no remote copies, remote signals or barrier semaphores. Data moves between devices by JAX's collectives and lax.ppermute only.
A program may use at most 128 MiB of HBM per device.

v0:
```python
import jax
import jax.numpy as jnp
from jax import lax
from jax.sharding import PartitionSpec as P

FF = 1408
EXPERTS = 32
TOP = 2
QUART = 4
WINDOW_KEYS = 128
MOST = 12


def carried_in(x, axis, combine, identity):
    peers, here = (lax.axis_size(axis), lax.axis_index(axis))
    everything = jax.tree.map(lambda part: lax.all_gather(part, axis), x)
    start = jax.tree.map(
        lambda part, zero: jnp.broadcast_to(jnp.asarray(zero, part.dtype), part.shape), x, identity
    )

    def turn(k, before):
        reached = k < here
        new = combine(before, jax.tree.map(lambda part: part[k], everything))
        return jax.tree.map(lambda a, b: jnp.where(reached, a, b), new, before)

    return lax.fori_loop(0, peers, turn, start)


def from_root(value, axis, source):
    kept = jnp.where(lax.axis_index(axis) == source, value, 0).astype(value.dtype)
    return lax.psum(kept, axis)


def passed_along(x, axis, by):
    peers = lax.axis_size(axis)
    pairs = [(i, i + by) for i in range(peers) if 0 <= i + by < peers]
    return lax.ppermute(x, axis, pairs)


def chain_step(earlier, later_part):
    decay_early, state_early = earlier
    decay_late, state_late = later_part
    return (decay_early * decay_late, decay_late[:, None, None] * state_early + state_late)


def expert_blocks(received, up_blocks, down_blocks):
    block_count = up_blocks.shape[1]
    feature_width = received.shape[-1]
    token_rows = received.reshape(block_count, -1, feature_width)
    hidden = jnp.einsum("brd,dbh->brh", token_rows, up_blocks, preferred_element_type=jnp.float32)
    hidden = jax.nn.silu(hidden).astype(jnp.bfloat16)
    partial_out = jnp.einsum(
        "brh,bhd->brd", hidden, down_blocks, preferred_element_type=jnp.float32
    )
    return partial_out.astype(jnp.bfloat16).reshape(received.shape)


def per_device(
    queries, key_tensor, value_tensor, decay_logarithm, lin_gain, routes, route_weight, w_up, w_down
):
    tok_count = queries.shape[0]
    model_width = queries.shape[1]
    kv_heads = decay_logarithm.shape[0]
    head_dim = key_tensor.shape[1] // kv_heads
    group_extent = model_width // (kv_heads * head_dim)
    scale_multiplier = head_dim ** (-0.5)
    hi_prec = lax.Precision.HIGHEST
    query_single = queries.astype(jnp.float32).reshape(tok_count, kv_heads, group_extent, head_dim)
    key_single = (
        key_tensor.astype(jnp.float32).reshape(tok_count, kv_heads, head_dim) * scale_multiplier
    )
    value_single = value_tensor.astype(jnp.float32).reshape(tok_count, kv_heads, head_dim)
    cum_decay = jnp.cumsum(decay_logarithm, axis=1)
    end_decay = cum_decay[:, -1]
    position = jnp.arange(tok_count)
    causal = position[:, None] >= position[None, :]
    gap_decay = cum_decay[:, :, None] - cum_decay[:, None, :]
    weight_mask = jnp.where(causal[None], jnp.exp(jnp.where(causal[None], gap_decay, 0.0)), 0.0)
    inner_scores = (
        jnp.einsum("thgd,shd->hgts", query_single, key_single, precision=hi_prec)
        * weight_mask[:, None]
    )
    inner_out = jnp.einsum("hgts,shd->thgd", inner_scores, value_single, precision=hi_prec)
    tail_weight = jnp.exp(end_decay[:, None] - cum_decay)
    local_state = jnp.einsum(
        "shd,she->hde", key_single * tail_weight.T[:, :, None], value_single, precision=hi_prec
    )
    own_part = (jnp.exp(end_decay), local_state)
    identity_part = (
        jnp.ones((kv_heads,), jnp.float32),
        jnp.zeros((kv_heads, head_dim, head_dim), jnp.float32),
    )
    group_before = carried_in(own_part, "narrow", chain_step, identity_part)
    group_whole = chain_step(group_before, own_part)
    group_whole = (
        from_root(group_whole[0], "narrow", lax.axis_size("narrow") - 1),
        from_root(group_whole[1], "narrow", lax.axis_size("narrow") - 1),
    )
    outer_before = carried_in(group_whole, "wide", chain_step, identity_part)
    incoming = chain_step(outer_before, group_before)
    carried = (
        jnp.einsum("thgd,hde->thge", query_single, incoming[1], precision=hi_prec)
        * jnp.exp(cum_decay).T[:, :, None, None]
    )
    linear_heads = (inner_out + carried).reshape(tok_count, -1, head_dim)
    mean_square = jnp.mean(linear_heads * linear_heads, axis=2, keepdims=True)
    normed = (linear_heads / jnp.sqrt(mean_square + 1e-06)).reshape(
        tok_count, model_width
    ) * lin_gain
    prev_keys, prev_values = passed_along((key_tensor, value_tensor), ("wide", "narrow"), 1)
    all_keys = jnp.concatenate([prev_keys, key_tensor], axis=0).reshape(-1, kv_heads, head_dim)
    all_values = jnp.concatenate([prev_values, value_tensor], axis=0).reshape(
        -1, kv_heads, head_dim
    )
    query_bfloat = queries.reshape(tok_count, kv_heads, group_extent, head_dim)
    raw_scores = (
        jnp.einsum("thgd,shd->hgts", query_bfloat, all_keys, preferred_element_type=jnp.float32)
        * scale_multiplier
    )
    key_pos = jnp.arange(WINDOW_KEYS + tok_count) - WINDOW_KEYS
    distance = position[:, None] - key_pos[None, :]
    device_index = lax.axis_index(("wide", "narrow"))
    allowed = (
        (distance >= 0) & (distance < WINDOW_KEYS) & ((key_pos[None, :] >= 0) | (device_index > 0))
    )
    masked = jnp.where(allowed[None, None], raw_scores, -jnp.inf)
    row_max = jnp.max(masked, axis=3, keepdims=True)
    expo_scores = jnp.exp(masked - row_max)
    probs = (expo_scores / jnp.sum(expo_scores, axis=3, keepdims=True)).astype(jnp.bfloat16)
    window_out = jnp.einsum(
        "hgts,shd->thgd", probs, all_values, preferred_element_type=jnp.float32
    ).reshape(tok_count, model_width)
    attn = (normed + window_out).astype(jnp.bfloat16)
    wide_count = lax.axis_size("wide")
    block_units = FF // QUART
    local_blocks = EXPERTS * QUART // wide_count
    up_blocks = w_up.reshape(model_width, local_blocks, block_units)
    down_blocks = w_down.reshape(local_blocks, block_units, model_width)
    flat_routes = routes.reshape(-1)
    onehot = (flat_routes[:, None] == jnp.arange(EXPERTS)[None, :]).astype(jnp.int32)
    earlier_count = jnp.cumsum(onehot, axis=0) - onehot
    slot_rank = jnp.sum(earlier_count * onehot, axis=1).reshape(routes.shape)[:, :, None]
    virtual = routes[:, :, None] * QUART + jnp.arange(QUART)[None, None, :]
    target = virtual // local_blocks
    local_slot = virtual % local_blocks
    total_slots = local_blocks * wide_count * MOST
    slot_index = (local_slot * wide_count + target) * MOST + slot_rank
    layout = (local_blocks, wide_count, MOST, model_width)
    slot_flat = slot_index.reshape(-1)
    token_ids = jnp.broadcast_to(
        jnp.arange(tok_count, dtype=jnp.int32)[:, None, None], slot_index.shape
    ).reshape(-1)
    source_row = jnp.full((total_slots,), tok_count, jnp.int32).at[slot_flat].set(token_ids)
    attn_padded = jnp.concatenate([attn, jnp.zeros((1, model_width), jnp.bfloat16)], axis=0)
    send_rows = attn_padded[source_row].reshape(layout)
    computed = expert_blocks(
        lax.all_to_all(send_rows, "wide", split_axis=1, concat_axis=1, tiled=True),
        up_blocks,
        down_blocks,
    )
    returned = lax.all_to_all(computed, "wide", split_axis=1, concat_axis=1, tiled=True)
    picked = returned.reshape(total_slots, model_width)[slot_flat].reshape(
        tok_count, TOP, QUART, model_width
    )
    block_sum = jnp.sum(picked, axis=2, dtype=jnp.float32)
    moe = jnp.sum(block_sum * route_weight[:, :, None], axis=1)
    return (attn.astype(jnp.float32) + moe).astype(jnp.bfloat16)


def solution(mesh):
    in_specs = (
        P(("wide", "narrow"), None),
        P(("wide", "narrow"), None),
        P(("wide", "narrow"), None),
        P(None, ("wide", "narrow")),
        P(),
        P(("wide", "narrow"), None),
        P(("wide", "narrow"), None),
        P(None, "wide"),
        P("wide", None),
    )
    out_specs = P(("wide", "narrow"), None)
    return jax.shard_map(
        per_device, mesh=mesh, in_specs=in_specs, out_specs=out_specs, check_vma=False
    )
```

profile of v0, /device:TPU:105, one launch (start us, length us, event | category | flops | bytes accessed | tf_op | source)
XLA Modules:
  0.0 932.7 jit_solution(6233057932366140087)
XLA Ops:
  10.0 11.5 %all-gather.1 = f32[8,128,128]{2,1,0:T(8,128)S(1)} all-gather(f32[2,128,128]{2,1,0:T(8,128)S(1)} %fusion.31), channel_id=3, replica_groups=mesh['wide'=128,'narrow'=4] {'narrow'}, dimensions={0}, use_global_device_ids=true | all-gather | bytes 655360 | tf_op jit(solution)/shard_map/all_gather | solution.py:16
  23.6 6.9 all-reduce.1
  32.0 56.9 %all-reduce.4.cloned.1.call-done = f32[1,2,128,128]{3,2,1,0:T(8,128)} async-done(((f32[1,2,128,128]{3,2,1,0:T(8,128)}), f32[1,2,128,128]{3,2,1,0:T(8,128)}) %all-reduce.4.cloned.1.call-update) | async-done | bytes 131088 | tf_op jit(solution)/shard_map/psum | solution.py:31
  91.3 3.4 collective-permute-start.1
  94.7 10.9 %psum.14 = f32[1,2]{1,0:T(1,128)S(1)} all-reduce(f32[1,2]{1,0:T(1,128)S(1)} %get-tuple-element.280), channel_id=1, replica_groups=mesh['wide'=128,'narrow'=4] {'narrow'}, use_global_device_ids=true, to_apply=%region_3.4 | all-reduce | flops 2 | bytes 16 | tf_op jit(solution)/shard_map/psum | solution.py:31
  108.4 4.3 scatter_custom_fusion
  112.8 44.2 %all-gather.2 = f32[128,1,2]{2,1,0:T(1,128)S(1)} all-gather(f32[1,1,2]{2,1,0:T(1,128)S(1)} %bitcast.157), channel_id=1, replica_groups=mesh['wide'=128,'narrow'=4] {'wide'}, dimensions={0}, use_global_device_ids=true | all-gather | bytes 1032 | tf_op jit(solution)/shard_map/all_gather | solution.py:16
  161.8 2.9 fusion.13
  166.3 26.6 %all-gather.5.cloned.1.call-done = f32[128,2,128,128]{3,2,1,0:T(8,128)} async-done(((f32[1,2,128,128]{3,2,1,0:T(8,128)}), f32[128,2,128,128]{3,2,1,0:T(8,128)}) %all-gather.5.cloned.1.call-update) | async-done | bytes 16777232 | tf_op jit(solution)/shard_map/all_gather | solution.py:16
  192.9 132.3 %while.31 = (s32[]{:T(128)}, f32[2,128,128]{2,1,0:T(8,128)S(1)}, s32[]{:T(128)}, f32[128,2]{1,0:T(8,128)S(1)}, f32[128,2,128,128]{3,2,1,0:T(8,128)}, /*index=5*/s32[]{:T(128)}, s32[]{:T(128)}) while((s32[]{:T(128)}, f32[2,128,128]{2,1,0:T(8,128)S(1)}, s32[]{:T(128)}, f32[128,2]{1,0:T(8,128)S(1)}, f32[128,2,128,128]{3,2,1,0:T(8,128)}, ...), condition=%wide.region_6.7_spmd.clone, body=%wide.region_5.6_spmd.clone.sunk | while | flops 131076 | bytes 393345 | solution.py:26
  325.1 3.0 multiply_reduce_fusion.1
  333.8 7.1 gather_fusion
  340.9 10.6 %reshape.252 = bf16[1,128,12,2048]{3,2,1,0:T(8,128)(2,1)} reshape(bf16[1536,2048]{1,0:T(8,128)(2,1)} %gather_fusion) | data formatting | bytes 12582912 | tf_op jit(solution)/shard_map/reshape | solution.py:155
  351.5 206.1 %all_to_all.10 = bf16[1,128,12,2048]{3,2,0,1:T(8,128)(2,1)} all-to-all(bf16[1,128,12,2048]{3,2,0,1:T(8,128)(2,1)} %bitcast.141), channel_id=1, replica_groups=mesh['wide'=128,'narrow'=4] {'wide'}, dimensions={1} | all-to-all | bytes 12582912 | tf_op jit(solution)/shard_map/all_to_all | solution.py:157
  557.6 10.8 %reshape.253 = bf16[1536,2048]{1,0:T(8,128)(2,1)} reshape(bf16[1,128,12,2048]{3,2,0,1:T(8,128)(2,1)} %all_to_all.10) | data formatting | bytes 12582912 | tf_op jit(solution)/shard_map/reshape.3
  568.4 11.2 %convolution_convert_fusion = bf16[1536,2048]{1,0:T(8,128)(2,1)} fusion(bf16[352,2048]{1,0:T(8,128)(2,1)S(1)} %copy-done, bf16[1536,2048]{1,0:T(8,128)(2,1)} %reshape.253, bf16[2048,352]{0,1:T(8,128)(2,1)S(1)} %copy-done.10), kind=kOutput, calls=%fused_computation.12 | convolution fusion | flops 4435034112 | bytes 15466496 | tf_op jit(solution)/shard_map/brh,bhd->brd/dot_general | solution.py:52
  579.6 10.6 %reshape.254 = bf16[1,128,12,2048]{3,2,1,0:T(8,128)(2,1)} reshape(bf16[1536,2048]{1,0:T(8,128)(2,1)} %convolution_convert_fusion) | data formatting | bytes 12582912 | tf_op jit(solution)/shard_map/reshape | solution.py:55
  590.1 24.0 %all-to-all-start.1 = ((bf16[1,128,12,2048]{3,2,0,1:T(8,128)(2,1)}), bf16[1,128,12,2048]{3,2,0,1:T(8,128)(2,1)}, u32[]{:S(2)}, u32[]{:S(2)}) async-start(bf16[1,128,12,2048]{3,2,0,1:T(8,128)(2,1)} %bitcast.140), calls=%async_computation.1 | async-start | bytes 16777216 | tf_op jit(solution)/shard_map/all_to_all | solution.py:161
  614.9 264.6 %all-to-all-done.1 = bf16[1,128,12,2048]{3,2,0,1:T(8,128)(2,1)} async-done(((bf16[1,128,12,2048]{3,2,0,1:T(8,128)(2,1)}), bf16[1,128,12,2048]{3,2,0,1:T(8,128)(2,1)}, u32[]{:S(2)}, u32[]{:S(2)}) %all-to-all-start.1) | async-done | bytes 6291488 | tf_op jit(solution)/shard_map/all_to_all | solution.py:161
  879.4 10.7 %reshape.255 = bf16[1536,2048]{1,0:T(8,128)(2,1)} reshape(bf16[1,128,12,2048]{3,2,0,1:T(8,128)(2,1)} %all-to-all-done.1) | data formatting | bytes 12582912 | tf_op jit(solution)/shard_map/reshape | solution.py:162
  890.1 12.4 %gather_fusion.1 = bf16[1024,2048]{1,0:T(8,128)(2,1)} fusion(bf16[1536,2048]{1,0:T(8,128)(2,1)} %reshape.255, s32[1024]{0:T(1024)S(1)} %broadcast_clamp_fusion), kind=kCustom, calls=%fused_computation.1 | custom fusion | bytes 8392704 | tf_op jit(solution)/shard_map/gather | solution.py:162
  902.6 8.3 reshape.258
  910.9 9.9 %reduce_sum.48 = f32[128,2,2048]{2,1,0:T(2,128)S(1)} reduce(f32[128,2,4,2048]{3,2,1,0:T(4,128)} %reshape.258, f32[]{:T(128)} %constant.109.clone.1), dimensions={2}, to_apply=%region_14.15 | reduce | flops 1572864 | bytes 10485764 | tf_op jit(solution)/shard_map/reduce_sum | solution.py:165
  920.8 4.1 multiply_reduce_fusion
  (352 shorter events, 153.7 us)
Async XLA Ops:
  6.5 561.9 %copy-start = (bf16[352,2048]{1,0:T(8,128)(2,1)S(1)}, bf16[352,2048]{1,0:T(8,128)(2,1)}, u32[]{:S(2)}) copy-start(bf16[352,2048]{1,0:T(8,128)(2,1)} %param.21) | copy-start | bytes 4325380
  6.5 84.6 %copy-start.4 = (bf16[128,256]{1,0:T(8,128)(2,1)S(1)}, bf16[128,256]{1,0:T(8,128)(2,1)}, u32[]{:S(2)}) copy-start(bf16[128,256]{1,0:T(8,128)(2,1)} %param.14) | copy-start | bytes 196612
  6.5 82.4 %copy-start.5 = (bf16[128,256]{1,0:T(8,128)(2,1)S(1)}, bf16[128,256]{1,0:T(8,128)(2,1)}, u32[]{:S(2)}) copy-start(bf16[128,256]{1,0:T(8,128)(2,1)} %param.15) | copy-start | bytes 196612
  6.5 82.4 %all-reduce.4.cloned.1.call-start = ((), (), s32[]{:S(2)}) async-start(), calls=%async_computation.2 | async-start | bytes 262144 | tf_op jit(solution)/shard_map/psum | solution.py:31
  7.9 97.7 %copy-start.8 = (s32[128,2]{0,1:T(2,128)S(1)}, s32[128,2]{0,1:T(2,128)}, u32[]{:S(2)}) copy-start(s32[128,2]{0,1:T(2,128)} %param.18) | copy-start | bytes 3076
  8.9 97.2 %copy-start.6 = (bf16[128,2048]{1,0:T(8,128)(2,1)S(1)}, bf16[128,2048]{1,0:T(8,128)(2,1)}, u32[]{:S(2)}) copy-start(bf16[128,2048]{1,0:T(8,128)(2,1)} %param.13) | copy-start | bytes 1572868
  31.9 160.9 %all-gather.5.cloned.1.call-start = ((), (), s32[]{:S(2)}) async-start(), calls=%async_computation.3 | async-start | bytes 16908288 | tf_op jit(solution)/shard_map/all_gather | solution.py:16
  88.9 70.5 %collective-permute-start = (bf16[128,256]{1,0:T(8,128)(2,1)S(1)}, bf16[128,256]{1,0:T(8,128)(2,1)S(1)}, u32[]{:S(2)}, u32[]{:S(2)}) collective-permute-start(bf16[128,256]{1,0:T(8,128)(2,1)S(1)} %copy-done.5), channel_id=1, source_target_pairs={{0,1},{1,2},{2,3},{3,4},{4,5},{5,6},{6,7},{7,8},{8,9},{9,10},{10,1... | collective-permute-start | bytes 196616 | tf_op jit(solution)/shard_map/ppermute | solution.py:37
  91.3 68.3 %collective-permute-start.1 = (bf16[128,256]{0,1:T(8,128)(2,1)S(1)}, bf16[128,256]{0,1:T(8,128)(2,1)S(1)}, u32[]{:S(2)}, u32[]{:S(2)}) collective-permute-start(bf16[128,256]{0,1:T(8,128)(2,1)S(1)} %copy.102), channel_id=1, source_target_pairs={{0,1},{1,2},{2,3},{3,4},{4,5},{5,6},{6,7},{7,8},{8,9},{9,10},{10,1... | collective-permute-start | bytes 196616 | tf_op jit(solution)/shard_map/ppermute | solution.py:37
  328.1 3.0 copy-start.7
  332.9 0.8 copy-start.2
  557.6 10.8 %copy-start.10 = (bf16[2048,352]{0,1:T(8,128)(2,1)S(1)}, bf16[2048,352]{0,1:T(8,128)(2,1)}, u32[]{:S(2)}) copy-start(bf16[2048,352]{0,1:T(8,128)(2,1)} %param.20) | copy-start | bytes 4325380
  590.1 24.0 %copy-start.9 = (f32[128,2]{0,1:T(2,128)S(1)}, f32[128,2]{0,1:T(2,128)}, u32[]{:S(2)}) copy-start(f32[128,2]{0,1:T(2,128)} %param.19) | copy-start | bytes 3076
  590.1 289.3 %all-to-all-start.1 = ((bf16[1,128,12,2048]{3,2,0,1:T(8,128)(2,1)}), bf16[1,128,12,2048]{3,2,0,1:T(8,128)(2,1)}, u32[]{:S(2)}, u32[]{:S(2)}) async-start(bf16[1,128,12,2048]{3,2,0,1:T(8,128)(2,1)} %bitcast.140), calls=%async_computation.1 | async-start | bytes 16777216 | tf_op jit(solution)/shard_map/all_to_all | solution.py:161
  910.9 14.9 %copy-start.1 = (bf16[352,2048]{1,0:T(8,128)(2,1)S(1)}, bf16[352,2048]{1,0:T(8,128)(2,1)}, u32[]{:S(2)}) copy-start(bf16[352,2048]{1,0:T(8,128)(2,1)} %param.21) | copy-start | bytes 4325380
  920.8 4.1 copy-start.3
Sparse Core Ops, SparseCore 0:
  32.0 56.8 all-reduce.3
  92.0 100.7 all-gather.4
where the time goes:
time: 937 us; the launch traced here: 933 us
  waiting for transfers between devices  348 us (37%)
  blocking collectives  280 us (30%)
  other arithmetic  147 us (16%)
  local copies, waits for them, and re-layouts  86.6 us (9%)
  starting transfers between devices  29.7 us (3%)
  matrix products  22.6 us (2%)
  between operations  14.5 us (2%)
    all_to_all x1, waiting for transfers between devices, per_device(): lax.all_to_all(computed, 'wide', split_axis=1, concat_axis=1, tiled=True)  265 us
    all_to_all x1, blocking collectives, per_device(): lax.all_to_all(send_rows, 'wide', split_axis=1, concat_axis=1, tiled=True)  206 us
    select_n x136, other arithmetic, turn(): return jax.tree.map(lambda a, b: jnp.where(reached, a, b), new, before)  127 us
    psum x1, waiting for transfers between devices, from_root(): return lax.psum(kept, axis)  56.9 us
    all_gather x2, blocking collectives, carried_in(): everything = jax.tree.map(lambda part: lax.all_gather(part, axis), x)  55.7 us
    all_gather x1, waiting for transfers between devices, carried_in(): everything = jax.tree.map(lambda part: lax.all_gather(part, axis), x)  26.6 us
    all_to_all x1, starting transfers between devices, per_device(): lax.all_to_all(computed, 'wide', split_axis=1, concat_axis=1, tiled=True)  24 us
  transfers between devices with their start and end apart: 5, of which 3 were waited for; matrix products, arithmetic and copies ran while one was open for 2% of the time, Pallas kernels for 0%

commit v1 on v0

v1 whole, which is shorter than its diff:
```python
import jax
import jax.numpy as jnp
from jax import lax
from jax.experimental import pallas as pl
from jax.experimental.pallas import tpu as pltpu
from jax.sharding import PartitionSpec as P


EXPERTS = 32
QUART = 4
MOST = 12
TOK = 128
HEADS = 16
HEAD = 128
KV = 2
GROUP = HEADS // KV
WIDTH = HEADS * HEAD
UNITS = 352
PADDED = 768
PIECE = 176
PITCH = 17
CHUNK = 96
SLOTS = EXPERTS * MOST
SCALE = HEAD ** (-0.5)
BOTH = ("wide", "narrow")
F32 = jnp.float32
BF16 = jnp.bfloat16
GROUPED = True


def dot(a, b, lhs=1, rhs=0):
    return lax.dot_general(a, b, (((lhs,), (rhs,)), ((), ())), preferred_element_type=F32)


def iota(shape, dim):
    return lax.broadcasted_iota(jnp.int32, shape, dim)


def split(x):
    high = x.astype(BF16)
    return high, (x - high.astype(F32)).astype(BF16)


def decay_sums(decay_ref, head):
    total = jnp.broadcast_to(decay_ref[head : head + 1, :], (8, TOK))
    lane = iota((8, TOK), 1)
    for by in (1, 2, 4, 8, 16, 32, 64):
        total = total + jnp.where(lane >= by, pltpu.roll(total, by, 1), 0.0)
    row = jnp.broadcast_to(total[0:1, :], (TOK, TOK))
    same = iota((TOK, TOK), 0) == iota((TOK, TOK), 1)
    column = jnp.sum(jnp.where(same, row, 0.0), axis=1, keepdims=True)
    return row, column


def state_kernel(key_ref, value_ref, decay_ref, message_ref, pair_ref):
    lane = iota((HEAD, HEAD), 1)
    for head in range(KV):
        cols = slice(head * HEAD, (head + 1) * HEAD)
        row, column = decay_sums(decay_ref, head)
        last = row[:, TOK - 1 : TOK]
        weighted = key_ref[:, cols].astype(F32) * jnp.exp(last - column)
        high, low = split(weighted)
        values = value_ref[:, cols]
        state = dot(
            jnp.concatenate([high, low], axis=0), jnp.concatenate([values, values], axis=0), 0, 0
        )
        fade = jnp.exp(jnp.broadcast_to(last, (HEAD, HEAD)))
        message_ref[head * HEAD : (head + 1) * HEAD, :] = jnp.where(lane < 64, state, fade)
        message_ref[256 + head * HEAD : 256 + (head + 1) * HEAD, :] = jnp.where(
            lane < 64, pltpu.roll(state, 64, 1), fade
        )
    pair_ref[:TOK, :] = key_ref[...]
    pair_ref[TOK:, :] = value_ref[...]


def prefix_kernel(message_ref, before_ref):
    count = message_ref.shape[0]
    shape = (count, 128)
    first = iota(shape, 1) < 64
    place = iota(shape, 0)
    neutral = jnp.where(first, 0.0, 1.0)
    run = message_ref[...]
    by = 1
    while by < count:
        earlier = jnp.where(place >= by, pltpu.roll(run, by, 0), neutral)
        fade = jnp.where(first, pltpu.roll(run, 64, 1), run)
        run = earlier * fade + jnp.where(first, run, 0.0)
        by *= 2
    before_ref[...] = jnp.where(place >= 1, pltpu.roll(run, 1, 0), 0.0)


def local_kernel(
    started_ref, query_ref, key_ref, value_ref, prev_ref, decay_ref, window_ref, inner_ref
):
    seen = iota((TOK, TOK), 1) <= iota((TOK, TOK), 0)
    usable = jnp.logical_or(seen, jnp.broadcast_to(started_ref[0] > 0, (TOK, TOK)))
    for head in range(KV):
        cols = slice(head * HEAD, (head + 1) * HEAD)
        row, column = decay_sums(decay_ref, head)
        weight = jnp.where(seen, jnp.exp(jnp.where(seen, column - row, 0.0)), 0.0)
        keys = jnp.concatenate([key_ref[:, cols], prev_ref[:TOK, cols]], axis=0)
        own = value_ref[:, cols]
        values = jnp.concatenate([own, prev_ref[TOK:, cols]], axis=0)
        twice = jnp.concatenate([own, own], axis=0)

        def one(j, carry):
            here = pl.ds(pl.multiple_of((head * GROUP + j) * HEAD, HEAD), HEAD)
            scores = dot(query_ref[:, here], keys, 1, 1)
            now, prev = scores[:, :TOK], scores[:, TOK:]
            high, low = split(now * weight)
            inner_ref[:, here] = dot(jnp.concatenate([high, low], axis=1), twice)
            masked = jnp.where(usable, jnp.where(seen, now, prev) * SCALE, -jnp.inf)
            expo = jnp.exp(masked - jnp.max(masked, axis=1, keepdims=True))
            probs = expo / jnp.sum(expo, axis=1, keepdims=True)
            both = jnp.concatenate(
                [jnp.where(seen, probs, 0.0), jnp.where(seen, 0.0, probs)], axis=1
            )
            window_ref[:, here] = dot(both.astype(BF16), values)
            return carry

        lax.fori_loop(0, GROUP, one, 0, unroll=2)


def finish_kernel(
    slot_ref, query_ref, before_ref, decay_ref, gain_ref, window_ref, inner_ref, attn_ref, send_ref, rows_ref
):
    lane = iota((HEAD, HEAD), 1)
    send_ref[...] = jnp.zeros(send_ref.shape, BF16)
    for head in range(KV):
        _, column = decay_sums(decay_ref, head)
        left = before_ref[head * HEAD : (head + 1) * HEAD, :]
        right = before_ref[256 + head * HEAD : 256 + (head + 1) * HEAD, :]
        state = jnp.where(lane < 64, left, pltpu.roll(right, 64, 1))
        halves = jnp.concatenate(split(state), axis=1)
        fade = jnp.exp(column)

        def one(j, carry):
            number = head * GROUP + j
            here = pl.ds(pl.multiple_of(number * HEAD, HEAD), HEAD)
            product = dot(query_ref[:, here], halves)
            carried = (product[:, :HEAD] + product[:, HEAD:]) * fade
            linear = (carried + inner_ref[:, here]) * SCALE
            mean = jnp.mean(linear * linear, axis=1, keepdims=True)
            normed = linear / jnp.sqrt(mean + 1e-06) * gain_ref[:, here]
            rows_ref[pl.ds(number, TOK, stride=PITCH), :] = normed + window_ref[:, here]
            return carry

        lax.fori_loop(0, GROUP, one, 0, unroll=2)

    def place(t, carry):
        row = rows_ref[pl.ds(t * PITCH, HEADS), :].astype(BF16)
        attn_ref[t] = row
        send_ref[slot_ref[2 * t]] = row
        send_ref[slot_ref[2 * t + 1]] = row
        return carry

    lax.fori_loop(0, TOK, place, 0, unroll=8)


def pick_kernel(plane_ref, up_ref, down_ref, piece_ref, sem):
    plane = plane_ref[0]
    rows = pl.ds(pl.multiple_of(lax.rem(plane, 2) * PIECE, PIECE), PIECE)

    @pl.when(plane < 2)
    def from_up():
        pltpu.make_async_copy(up_ref.at[rows, :], piece_ref, sem).start()

    @pl.when(plane >= 2)
    def from_down():
        pltpu.make_async_copy(down_ref.at[rows, :], piece_ref, sem).start()

    pltpu.make_async_copy(down_ref.at[rows, :], piece_ref, sem).wait()


def expert_kernel(plane_ref, recv_ref, *refs):
    sources, rest = refs[:12], refs[12:]
    out_ref, tiles_ref, rows_ref, x_ref, held_ref, hidden_ref, sems, tile_sems = rest
    plane = plane_ref[0]
    up_ref = held_ref.at[pl.ds(0, QUART * UNITS), :]
    down_ref = held_ref.at[pl.ds(QUART * UNITS, 2 * PADDED), :]
    down_at = QUART * UNITS
    arrivals = []
    for n in range(SLOTS // CHUNK):
        some = pl.ds(n * CHUNK, CHUNK)
        arrivals.append(
            pltpu.make_async_copy(recv_ref.at[some], tiles_ref.at[some], tile_sems.at[n])
        )
        arrivals[n].start()
    copies = []
    for n, at in enumerate((0, down_at, UNITS, down_at + UNITS)):
        copies.append(
            pltpu.make_async_copy(sources[n], held_ref.at[pl.ds(at, UNITS), :], sems.at[n])
        )
    for n in range(8):
        shard, step = n // 4, n % 4
        quarter = lax.rem(plane - step + 4, 4)
        at = jnp.where(
            quarter < 2,
            (2 + shard) * UNITS + quarter * PIECE,
            down_at + PADDED + shard * UNITS + (quarter - 2) * PIECE,
        )
        place = pl.ds(pl.multiple_of(at, PIECE // 11), PIECE)
        copies.append(
            pltpu.make_async_copy(sources[4 + n], held_ref.at[place, :], sems.at[4 + n])
        )
    for n in (0, 2, 1, 3, 4, 5, 6, 7, 8, 9, 10, 11):
        copies[n].start()
    for half in range(2):
        end = (half + 1) * PADDED
        down_ref[end - 64 : end, :] = jnp.zeros((64, WIDTH), BF16)
        hidden_ref[:, end - 128 : end] = jnp.zeros((SLOTS, 128), BF16)

    def unpack(t, carry):
        rows_ref[pl.ds(t * PITCH, HEADS), :] = tiles_ref[t].astype(F32)
        return carry

    for n in range(SLOTS // CHUNK):
        arrivals[n].wait()
        lax.fori_loop(n * CHUNK, (n + 1) * CHUNK, unpack, 0, unroll=16)
    for j in range(HEADS):
        x_ref[:, j * HEAD : (j + 1) * HEAD] = rows_ref[
            pl.ds(j, SLOTS, stride=PITCH), :
        ].astype(BF16)
    for half in range(2):
        for n in ((0, 2), (1, 3, 4, 5, 6, 7, 8, 9, 10, 11))[half]:
            copies[n].wait()
        for start, size in ((0, 256), (256, 256), (512, 192)):
            at = half * 2 * UNITS + start
            hidden = 0.5 * dot(x_ref[...], up_ref[at : at + size, :], 1, 1)
            hidden = hidden + hidden * jnp.tanh(hidden)
            at = half * PADDED + start
            hidden_ref[:, at : at + size] = hidden.astype(BF16)

    def columns(n, carry):
        here = pl.ds(pl.multiple_of(n * 256, 256), 256)
        result = dot(hidden_ref[...], down_ref[:, here])
        rows_ref[pl.ds(2 * n, SLOTS, stride=PITCH), :] = result[:, :HEAD]
        rows_ref[pl.ds(2 * n + 1, SLOTS, stride=PITCH), :] = result[:, HEAD:]
        return carry

    lax.fori_loop(0, WIDTH // 256, columns, 0, unroll=4)

    def pack(t, carry):
        tiles_ref[t] = rows_ref[pl.ds(t * PITCH, HEADS), :].astype(BF16)
        return carry

    leaving = []
    for n in range(SLOTS // CHUNK):
        lax.fori_loop(n * CHUNK, (n + 1) * CHUNK, pack, 0, unroll=16)
        some = pl.ds(n * CHUNK, CHUNK)
        leaving.append(pltpu.make_async_copy(tiles_ref.at[some], out_ref.at[some], tile_sems.at[n]))
        leaving[n].start()
    for one in leaving:
        one.wait()


def combine_kernel(slot_ref, gate_ref, back_ref, attn_ref, out_ref, rows_ref):
    def one(t, carry):
        moe = back_ref[slot_ref[2 * t]].astype(F32) * gate_ref[2 * t]
        moe = moe + back_ref[slot_ref[2 * t + 1]].astype(F32) * gate_ref[2 * t + 1]
        rows_ref[pl.ds(t * PITCH, HEADS), :] = attn_ref[t].astype(F32) + moe
        return carry

    lax.fori_loop(0, TOK, one, 0, unroll=8)
    for j in range(HEADS):
        out_ref[:, j * HEAD : (j + 1) * HEAD] = rows_ref[
            pl.ds(j, TOK, stride=PITCH), :
        ].astype(BF16)


VMEM = pl.BlockSpec(memory_space=pltpu.VMEM)
SMEM = pl.BlockSpec(memory_space=pltpu.SMEM)
FAR = pl.BlockSpec(memory_space=pltpu.HBM)


def call(kernel, outs, in_specs, scratch=(), flops=0, moved=0, exps=0, room=16, place=VMEM):
    shapes = [jax.ShapeDtypeStruct(shape, dtype) for shape, dtype in outs]
    return pl.pallas_call(
        kernel,
        out_shape=shapes if len(shapes) > 1 else shapes[0],
        in_specs=in_specs,
        out_specs=[place] * len(shapes) if len(shapes) > 1 else place,
        scratch_shapes=list(scratch),
        compiler_params=pltpu.CompilerParams(vmem_limit_bytes=room << 20),
        cost_estimate=pl.CostEstimate(flops=flops, bytes_accessed=moved, transcendentals=exps),
    )


def swapped(x, bit):
    peers = lax.axis_size("wide")
    return lax.ppermute(x, "wide", [(i, i ^ bit) for i in range(peers)])


def exchanged(x, axis):
    return lax.all_to_all(x, axis, split_axis=0, concat_axis=0, tiled=True)


def routed(rows):
    flat = rows.reshape(SLOTS * HEADS, HEAD)
    groups = [[e * QUART + q for e in range(EXPERTS)] for q in range(QUART)] if GROUPED else None
    traded = lax.all_to_all(
        flat, "wide", split_axis=0, concat_axis=0, tiled=True, axis_index_groups=groups
    )
    return traded.reshape(rows.shape)


def per_device(
    queries, key_tensor, value_tensor, decay_logarithm, lin_gain, routes, route_weight, w_up, w_down
):
    devices = lax.axis_size(BOTH)
    message, pair = call(
        state_kernel,
        [((devices, 128), F32), ((2 * TOK, KV * HEAD), BF16)],
        [VMEM] * 3,
        room=58,
        flops=1 << 24,
        moved=600_000,
    )(key_tensor, value_tensor, decay_logarithm)
    gathered = exchanged(message, BOTH)
    previous = lax.ppermute(pair, BOTH, [(i, i + 1) for i in range(devices - 1)])
    up = w_up.T
    plane = lax.axis_index("narrow").astype(jnp.int32).reshape(1)
    planes = lax.axis_size("narrow")
    piece = call(
        pick_kernel,
        [((PIECE, WIDTH), BF16)],
        [SMEM, FAR, FAR],
        [pltpu.SemaphoreType.DMA],
        room=58,
        moved=1_400_000,
    )(plane, up, w_down)
    pieces = [swapped(piece, 2)]
    for by in (1, 2, 3):
        around = [(i, (i + by) % planes) for i in range(planes)]
        pieces.append(lax.ppermute(pieces[0], "narrow", around))
    up_c, down_c = swapped(up, 1), swapped(w_down, 1)
    onward = [swapped(one, 1) for one in pieces]

    before = call(
        prefix_kernel, [((devices, 128), F32)], [VMEM], flops=1 << 22, moved=524_288
    )(gathered)
    before = exchanged(before, BOTH)

    flat = routes.reshape(-1)
    onehot = (flat[:, None] == jnp.arange(EXPERTS)[None, :]).astype(jnp.int32)
    rank = jnp.sum((jnp.cumsum(onehot, axis=0) - onehot) * onehot, axis=1)
    slots = flat * MOST + rank
    started = jnp.minimum(lax.axis_index(BOTH), 1).astype(jnp.int32).reshape(1)
    window, inner = call(
        local_kernel,
        [((TOK, WIDTH), F32)] * 2,
        [SMEM] + [VMEM] * 5,
        flops=1 << 29,
        moved=3_000_000,
        exps=1 << 18,
    )(started, queries, key_tensor, value_tensor, previous, decay_logarithm)
    attn, send = call(
        finish_kernel,
        [((TOK, HEADS, HEAD), BF16), ((SLOTS, HEADS, HEAD), BF16)],
        [SMEM] + [VMEM] * 6,
        [pltpu.VMEM((TOK * PITCH, HEAD), F32)],
        flops=1 << 28,
        moved=5_000_000,
    )(slots, queries, before, decay_logarithm, lin_gain.reshape(1, WIDTH), window, inner)

    received = routed(send)
    computed = call(
        expert_kernel,
        [((SLOTS, HEADS, HEAD), BF16)],
        [SMEM] + [FAR] * 13,
        [
            pltpu.VMEM((SLOTS, HEADS, HEAD), BF16),
            pltpu.VMEM((SLOTS * PITCH, HEAD), F32),
            pltpu.VMEM((SLOTS, WIDTH), BF16),
            pltpu.VMEM((QUART * UNITS + 2 * PADDED, WIDTH), BF16),
            pltpu.VMEM((SLOTS, 2 * PADDED), BF16),
            pltpu.SemaphoreType.DMA((12,)),
            pltpu.SemaphoreType.DMA((SLOTS // CHUNK,)),
        ],
        room=62,
        place=FAR,
        flops=4_500_000_000,
        moved=15_000_000,
        exps=1 << 19,
    )(plane, received, up, w_down, up_c, down_c, *pieces, *onward)
    back = routed(computed)
    return call(
        combine_kernel,
        [((TOK, WIDTH), BF16)],
        [SMEM] * 2 + [VMEM] * 2,
        [pltpu.VMEM((TOK * PITCH, HEAD), F32)],
        flops=1 << 20,
        moved=2_600_000,
    )(slots, route_weight.reshape(-1), back, attn)


def solution(mesh):
    rows = P(("wide", "narrow"), None)
    in_specs = (rows, rows, rows, P(None, ("wide", "narrow")), P(), rows, rows, P(None, "wide"), P("wide", None))
    return jax.shard_map(per_device, mesh=mesh, in_specs=in_specs, out_specs=rows, check_vma=False)
```

time: 937 us -> 256 us (0.27)
  the two profiles are of different devices: /device:TPU:105 before, /device:TPU:48 now
where the time goes in v1:
time: 256 us
  waiting for transfers between devices  135 us (53%)
  starting transfers between devices  81.8 us (32%)
  Pallas kernels  32.3 us (13%)
  local copies, waits for them, and re-layouts  5.47 us (2%)
    ppermute x7, waiting for transfers between devices, swapped(): return lax.ppermute(x, 'wide', [(i, i ^ bit) for i in range(peers)])  47.4 us
    all_to_all x2, waiting for transfers between devices, routed(): lax.all_to_all(flat, 'wide', split_axis=0, concat_axis=0, tiled=True, axi...  43.8 us
    all_to_all x2, starting transfers between devices, exchanged(): return lax.all_to_all(x, axis, split_axis=0, concat_axis=0, tiled=True)  32.9 us
    ppermute x3, waiting for transfers between devices, per_device(): pieces.append(lax.ppermute(pieces[0], 'narrow', around))  26.9 us
    all_to_all x2, starting transfers between devices, routed(): lax.all_to_all(flat, 'wide', split_axis=0, concat_axis=0, tiled=True, axi...  20.4 us
    all_to_all x2, waiting for transfers between devices, exchanged(): return lax.all_to_all(x, axis, split_axis=0, concat_axis=0, tiled=True)  16.8 us
    ppermute x7, starting transfers between devices, swapped(): return lax.ppermute(x, 'wide', [(i, i ^ bit) for i in range(peers)])  15.4 us
    pallas_call x1, Pallas kernels, per_device(): call(expert_kernel, [((SLOTS, HEADS, HEAD), BF16)], [SMEM] + [FAR] * 13,...  12.9 us
  transfers between devices with their start and end apart: 15, of which 6 were waited for; matrix products, arithmetic and copies ran while one was open for 1% of the time, Pallas kernels for 4%

profile of v1, /device:TPU:48, one launch (start us, length us, event | category | flops | bytes accessed | tf_op | source)
XLA Modules:
  0.0 255.6 jit_solution(13562477289835275179)
XLA Ops:
  0.0 2.6 %shard_map.91 = (f32[512,128]{1,0:T(8,128)}, bf16[256,256]{1,0:T(8,128)(2,1)}) custom-call(bf16[128,256]{1,0:T(8,128)(2,1)} %key_ref.3, bf16[128,256]{1,0:T(8,128)(2,1)} %value_ref.3, f32[2,128]{1,0:T(2,128)} %decay_ref.5), custom_call_target="tpu_custom_call" | custom-call | flops 16777216 | bytes 600000 | tf_op jit(solution)/shard_map/pallas_call | solution.py:311
  2.6 20.8 %all-to-all-start = ((f32[512,1,128]{2,1,0:T(1,128)}), f32[512,1,128]{2,1,0:T(1,128)S(1)}, u32[]{:S(2)}, u32[]{:S(2)}) async-start(f32[512,1,128]{2,1,0:T(1,128)} %bitcast.43), calls=%async_computation | async-start | bytes 524288 | tf_op jit(solution)/shard_map/all_to_all | solution.py:295
  23.4 3.4 %collective-permute-start = (bf16[256,256]{1,0:T(8,128)(2,1)}, bf16[256,256]{1,0:T(8,128)(2,1)S(1)}, u32[]{:S(2)}, u32[]{:S(2)}) collective-permute-start(bf16[256,256]{1,0:T(8,128)(2,1)} %get-tuple-element.12), channel_id=1, source_target_pairs={{0,1},{1,2},{2,3},{3,4},{4,5},{5,6},{6,7},{7,8},{8,9},{9,10},{10,1... | collective-permute-start | bytes 393224 | tf_op jit(solution)/shard_map/ppermute | solution.py:320
  27.7 9.7 %all-to-all-done = f32[512,1,128]{2,1,0:T(1,128)S(1)} async-done(((f32[512,1,128]{2,1,0:T(1,128)}), f32[512,1,128]{2,1,0:T(1,128)S(1)}, u32[]{:S(2)}, u32[]{:S(2)}) %all-to-all-start) | async-done | bytes 262176 | tf_op jit(solution)/shard_map/all_to_all | solution.py:295
  38.9 12.1 %all-to-all-start.1 = ((f32[512,1,128]{2,1,0:T(1,128)}), f32[512,1,128]{2,1,0:T(1,128)S(1)}, u32[]{:S(2)}, u32[]{:S(2)}) async-start(f32[512,1,128]{2,1,0:T(1,128)} %bitcast.6), calls=%async_computation.1 | async-start | bytes 524288 | tf_op jit(solution)/shard_map/all_to_all | solution.py:295
  52.2 5.6 %shard_map.93 = (f32[128,2048]{1,0:T(8,128)S(1)}, f32[128,2048]{1,0:T(8,128)S(1)}) custom-call(s32[1]{0:T(128)} %bitcast.9.started_ref, bf16[128,2048]{1,0:T(8,128)(2,1)S(1)} %copy-done, bf16[128,256]{1,0:T(8,128)(2,1)S(1)} %copy-done.1, bf16[128,256]{1,0:T(8,128)(2,1)S(1)} %copy-done.2, bf16[256,256]{1,0:T(8,128)(2,1)S(1)} %collective-permute-done.prev_ref, ...), custom_call_target="tpu_custom_call" | custom-call | flops 536870912 | bytes 3000000 | tf_op jit(solution)/shard_map/pallas_call | solution.py:349
  57.8 7.1 %all-to-all-done.1 = f32[512,1,128]{2,1,0:T(1,128)S(1)} async-done(((f32[512,1,128]{2,1,0:T(1,128)}), f32[512,1,128]{2,1,0:T(1,128)S(1)}, u32[]{:S(2)}, u32[]{:S(2)}) %all-to-all-start.1) | async-done | bytes 262176 | tf_op jit(solution)/shard_map/all_to_all | solution.py:295
  64.9 5.6 %shard_map.94 = (bf16[128,16,128]{2,1,0:T(8,128)(2,1)S(1)}, bf16[384,16,128]{2,1,0:T(8,128)(2,1)}) custom-call(s32[256]{0:T(256)S(1)} %multiply_add_fusion.slot_ref, bf16[128,2048]{1,0:T(8,128)(2,1)S(1)} %copy-done, f32[512,128]{1,0:T(8,128)S(1)} %bitcast.36, f32[2,128]{1,0:T(2,128)S(1)} %copy-done.4, f32[1,2048]{1,0:T(1,128)S(1)} %bitcast.38, ...), custom_call_target="tpu_custom_call" | custom-call | flops 268435456 | bytes 5000000 | tf_op jit(solution)/shard_map/pallas_call | solution.py:357
  70.6 8.1 %all-to-all-start.2 = ((bf16[32,192,128]{2,1,0:T(8,128)(2,1)}), bf16[32,192,128]{2,1,0:T(8,128)(2,1)}, u32[]{:S(2)}, u32[]{:S(2)}) async-start(bf16[32,192,128]{2,1,0:T(8,128)(2,1)} %bitcast.10), calls=%async_computation.2 | async-start | bytes 3145728 | tf_op jit(solution)/shard_map/all_to_all | solution.py:301
  78.7 2.1 shard_map.95
  80.8 3.0 %collective-permute-start.3 = (bf16[176,2048]{1,0:T(8,128)(2,1)}, bf16[176,2048]{1,0:T(8,128)(2,1)S(1)}, u32[]{:S(2)}, u32[]{:S(2)}) collective-permute-start(bf16[176,2048]{1,0:T(8,128)(2,1)} %shard_map.95), channel_id=1, source_target_pairs={{0,8},{4,12},{8,0},{12,4},{16,24},{20,28},{24,16},{28,20},{32,40},... | collective-permute-start | bytes 2162696 | tf_op jit(solution)/shard_map/ppermute | solution.py:291
  83.8 47.4 %collective-permute-done.3.refs_4_ = bf16[176,2048]{1,0:T(8,128)(2,1)S(1)} collective-permute-done((bf16[176,2048]{1,0:T(8,128)(2,1)}, bf16[176,2048]{1,0:T(8,128)(2,1)S(1)}, u32[]{:S(2)}, u32[]{:S(2)}) %collective-permute-start.3) | collective-permute-done | bytes 720928 | tf_op jit(solution)/shard_map/ppermute | solution.py:291
  131.2 3.5 %collective-permute-start.6 = (bf16[176,2048]{1,0:T(8,128)(2,1)S(1)}, bf16[176,2048]{1,0:T(8,128)(2,1)S(1)}, u32[]{:S(2)}, u32[]{:S(2)}) collective-permute-start(bf16[176,2048]{1,0:T(8,128)(2,1)S(1)} %collective-permute-done.3.refs_4_), channel_id=1, source_target_pairs={{0,3},{1,0},{2,1},{3,2},{4,7},{5,4},{6,5},{7,6},{8,11},{9,8},{10,9... | collective-permute-start | bytes 2162696 | tf_op jit(solution)/shard_map/ppermute | solution.py:335
  136.7 2.3 collective-permute-start.4
  139.0 2.1 collective-permute-start.2
  141.2 3.8 %collective-permute-start.5 = (bf16[176,2048]{1,0:T(8,128)(2,1)S(1)}, bf16[176,2048]{1,0:T(8,128)(2,1)S(1)}, u32[]{:S(2)}, u32[]{:S(2)}) collective-permute-start(bf16[176,2048]{1,0:T(8,128)(2,1)S(1)} %collective-permute-done.3.refs_4_), channel_id=1, source_target_pairs={{0,2},{1,3},{2,0},{3,1},{4,6},{5,7},{6,4},{7,5},{8,10},{9,11},{10,... | collective-permute-start | bytes 2162696 | tf_op jit(solution)/shard_map/ppermute | solution.py:335
  145.0 7.1 %collective-permute-done.6.refs_7_ = bf16[176,2048]{1,0:T(8,128)(2,1)S(1)} collective-permute-done((bf16[176,2048]{1,0:T(8,128)(2,1)S(1)}, bf16[176,2048]{1,0:T(8,128)(2,1)S(1)}, u32[]{:S(2)}, u32[]{:S(2)}) %collective-permute-start.6) | collective-permute-done | bytes 720928 | tf_op jit(solution)/shard_map/ppermute | solution.py:335
  154.0 19.8 %collective-permute-done.4.refs_5_ = bf16[176,2048]{1,0:T(8,128)(2,1)S(1)} collective-permute-done((bf16[176,2048]{1,0:T(8,128)(2,1)S(1)}, bf16[176,2048]{1,0:T(8,128)(2,1)S(1)}, u32[]{:S(2)}, u32[]{:S(2)}) %collective-permute-start.4) | collective-permute-done | bytes 720928 | tf_op jit(solution)/shard_map/ppermute | solution.py:335
  175.7 2.4 collective-permute-start.8
  178.2 2.1 collective-permute-start.9
  184.3 12.9 %shard_map.96 = bf16[384,16,128]{2,1,0:T(8,128)(2,1)} custom-call(s32[1]{0:T(128)} %bitcast.1.plane_ref, bf16[384,16,128]{2,1,0:T(8,128)(2,1)} %bitcast.11.recv_ref, bf16[352,2048]{1,0:T(8,128)(2,1)} %bitcast.41, bf16[352,2048]{1,0:T(8,128)(2,1)} %refs_1_.1, bf16[352,2048]{1,0:T(8,128)(2,1)} %copy-done.8, bf16[352,2048]{1,0:T(8,128)(2,1)} %copy-done.9, ...), custom_call_target="tpu_custom_call" | custom-call | flops 4499999744 | bytes 15000000 | tf_op jit(solution)/shard_map/pallas_call | solution.py:367
  197.2 12.4 %all-to-all-start.3 = ((bf16[32,192,128]{2,1,0:T(8,128)(2,1)}), bf16[32,192,128]{2,1,0:T(8,128)(2,1)S(1)}, u32[]{:S(2)}, u32[]{:S(2)}) async-start(bf16[32,192,128]{2,1,0:T(8,128)(2,1)} %bitcast.39), calls=%async_computation.3 | async-start | bytes 3145728 | tf_op jit(solution)/shard_map/all_to_all | solution.py:301
  209.8 43.8 %all-to-all-done.3 = bf16[32,192,128]{2,1,0:T(8,128)(2,1)S(1)} async-done(((bf16[32,192,128]{2,1,0:T(8,128)(2,1)}), bf16[32,192,128]{2,1,0:T(8,128)(2,1)S(1)}, u32[]{:S(2)}, u32[]{:S(2)}) %all-to-all-start.3) | async-done | bytes 1572896 | tf_op jit(solution)/shard_map/all_to_all | solution.py:301
  253.6 2.0 shard_map.97
  (59 shorter events, 13.4 us)
Async XLA Ops:
  0.0 52.1 %copy-start.1 = (bf16[128,256]{1,0:T(8,128)(2,1)S(1)}, bf16[128,256]{1,0:T(8,128)(2,1)}, u32[]{:S(2)}) copy-start(bf16[128,256]{1,0:T(8,128)(2,1)} %key_ref.3) | copy-start | bytes 196612
  0.0 52.1 %copy-start.2 = (bf16[128,256]{1,0:T(8,128)(2,1)S(1)}, bf16[128,256]{1,0:T(8,128)(2,1)}, u32[]{:S(2)}) copy-start(bf16[128,256]{1,0:T(8,128)(2,1)} %value_ref.3) | copy-start | bytes 196612
  0.0 52.1 %copy-start.4 = (f32[2,128]{1,0:T(2,128)S(1)}, f32[2,128]{1,0:T(2,128)}, u32[]{:S(2)}) copy-start(f32[2,128]{1,0:T(2,128)} %decay_ref.5) | copy-start | bytes 3076
  0.0 52.2 %copy-start = (bf16[128,2048]{1,0:T(8,128)(2,1)S(1)}, bf16[128,2048]{1,0:T(8,128)(2,1)}, u32[]{:S(2)}) copy-start(bf16[128,2048]{1,0:T(8,128)(2,1)} %query_ref.3) | copy-start | bytes 1572868
  2.6 34.8 %all-to-all-start = ((f32[512,1,128]{2,1,0:T(1,128)}), f32[512,1,128]{2,1,0:T(1,128)S(1)}, u32[]{:S(2)}, u32[]{:S(2)}) async-start(f32[512,1,128]{2,1,0:T(1,128)} %bitcast.43), calls=%async_computation | async-start | bytes 524288 | tf_op jit(solution)/shard_map/all_to_all | solution.py:295
  23.4 28.7 %collective-permute-start = (bf16[256,256]{1,0:T(8,128)(2,1)}, bf16[256,256]{1,0:T(8,128)(2,1)S(1)}, u32[]{:S(2)}, u32[]{:S(2)}) collective-permute-start(bf16[256,256]{1,0:T(8,128)(2,1)} %get-tuple-element.12), channel_id=1, source_target_pairs={{0,1},{1,2},{2,3},{3,4},{4,5},{5,6},{6,7},{7,8},{8,9},{9,10},{10,1... | collective-permute-start | bytes 393224 | tf_op jit(solution)/shard_map/ppermute | solution.py:320
  37.5 27.5 %copy-start.3 = (f32[2048]{0:T(1024)S(1)}, f32[2048]{0:T(1024)}, u32[]{:S(2)}) copy-start(f32[2048]{0:T(1024)} %param.13) | copy-start | bytes 24580
  38.9 26.0 %all-to-all-start.1 = ((f32[512,1,128]{2,1,0:T(1,128)}), f32[512,1,128]{2,1,0:T(1,128)S(1)}, u32[]{:S(2)}, u32[]{:S(2)}) async-start(f32[512,1,128]{2,1,0:T(1,128)} %bitcast.6), calls=%async_computation.1 | async-start | bytes 524288 | tf_op jit(solution)/shard_map/all_to_all | solution.py:295
  70.6 113.7 %all-to-all-start.2 = ((bf16[32,192,128]{2,1,0:T(8,128)(2,1)}), bf16[32,192,128]{2,1,0:T(8,128)(2,1)}, u32[]{:S(2)}, u32[]{:S(2)}) async-start(bf16[32,192,128]{2,1,0:T(8,128)(2,1)} %bitcast.10), calls=%async_computation.2 | async-start | bytes 3145728 | tf_op jit(solution)/shard_map/all_to_all | solution.py:301
  78.7 56.1 %copy-start.5 = (bf16[2048,352]{0,1:T(8,128)(2,1)S(1)}, bf16[2048,352]{0,1:T(8,128)(2,1)}, u32[]{:S(2)}) copy-start(bf16[2048,352]{0,1:T(8,128)(2,1)} %param.16) | copy-start | bytes 4325380
  78.7 60.3 %copy-start.6 = (bf16[352,2048]{1,0:T(8,128)(2,1)S(1)}, bf16[352,2048]{1,0:T(8,128)(2,1)}, u32[]{:S(2)}) copy-start(bf16[352,2048]{1,0:T(8,128)(2,1)} %refs_1_.1) | copy-start | bytes 4325380
  80.8 50.4 %collective-permute-start.3 = (bf16[176,2048]{1,0:T(8,128)(2,1)}, bf16[176,2048]{1,0:T(8,128)(2,1)S(1)}, u32[]{:S(2)}, u32[]{:S(2)}) collective-permute-start(bf16[176,2048]{1,0:T(8,128)(2,1)} %shard_map.95), channel_id=1, source_target_pairs={{0,8},{4,12},{8,0},{12,4},{16,24},{20,28},{24,16},{28,20},{32,40},... | collective-permute-start | bytes 2162696 | tf_op jit(solution)/shard_map/ppermute | solution.py:291
  131.2 53.0 %copy-start.10 = (bf16[176,2048]{1,0:T(8,128)(2,1)}, bf16[176,2048]{1,0:T(8,128)(2,1)S(1)}, u32[]{:S(2)}) copy-start(bf16[176,2048]{1,0:T(8,128)(2,1)S(1)} %collective-permute-done.3.refs_4_) | copy-start | bytes 2162692
  131.2 20.9 %collective-permute-start.6 = (bf16[176,2048]{1,0:T(8,128)(2,1)S(1)}, bf16[176,2048]{1,0:T(8,128)(2,1)S(1)}, u32[]{:S(2)}, u32[]{:S(2)}) collective-permute-start(bf16[176,2048]{1,0:T(8,128)(2,1)S(1)} %collective-permute-done.3.refs_4_), channel_id=1, source_target_pairs={{0,3},{1,0},{2,1},{3,2},{4,7},{5,4},{6,5},{7,6},{8,11},{9,8},{10,9... | collective-permute-start | bytes 2162696 | tf_op jit(solution)/shard_map/ppermute | solution.py:335
  134.8 45.5 %collective-permute-start.1 = (bf16[352,2048]{1,0:T(8,128)(2,1)S(1)}, bf16[352,2048]{1,0:T(8,128)(2,1)S(1)}, u32[]{:S(2)}, u32[]{:S(2)}) collective-permute-start(bf16[352,2048]{1,0:T(8,128)(2,1)S(1)} %bitcast.42), channel_id=1, source_target_pairs={{0,4},{4,0},{8,12},{12,8},{16,20},{20,16},{24,28},{28,24},{32,36},... | collective-permute-start | bytes 4325384 | tf_op jit(solution)/shard_map/ppermute | solution.py:291
  136.7 37.1 %collective-permute-start.4 = (bf16[176,2048]{1,0:T(8,128)(2,1)S(1)}, bf16[176,2048]{1,0:T(8,128)(2,1)S(1)}, u32[]{:S(2)}, u32[]{:S(2)}) collective-permute-start(bf16[176,2048]{1,0:T(8,128)(2,1)S(1)} %collective-permute-done.3.refs_4_), channel_id=1, source_target_pairs={{0,1},{1,2},{2,3},{3,0},{4,5},{5,6},{6,7},{7,4},{8,9},{9,10},{10,1... | collective-permute-start | bytes 2162696 | tf_op jit(solution)/shard_map/ppermute | solution.py:335
  139.0 41.3 %collective-permute-start.2 = (bf16[352,2048]{1,0:T(8,128)(2,1)S(1)}, bf16[352,2048]{1,0:T(8,128)(2,1)S(1)}, u32[]{:S(2)}, u32[]{:S(2)}) collective-permute-start(bf16[352,2048]{1,0:T(8,128)(2,1)S(1)} %copy-done.6), channel_id=1, source_target_pairs={{0,4},{4,0},{8,12},{12,8},{16,20},{20,16},{24,28},{28,24},{32,36},... | collective-permute-start | bytes 4325384 | tf_op jit(solution)/shard_map/ppermute | solution.py:291
  141.2 34.6 %collective-permute-start.5 = (bf16[176,2048]{1,0:T(8,128)(2,1)S(1)}, bf16[176,2048]{1,0:T(8,128)(2,1)S(1)}, u32[]{:S(2)}, u32[]{:S(2)}) collective-permute-start(bf16[176,2048]{1,0:T(8,128)(2,1)S(1)} %collective-permute-done.3.refs_4_), channel_id=1, source_target_pairs={{0,2},{1,3},{2,0},{3,1},{4,6},{5,7},{6,4},{7,5},{8,10},{9,11},{10,... | collective-permute-start | bytes 2162696 | tf_op jit(solution)/shard_map/ppermute | solution.py:335
  152.1 30.4 %copy-start.11 = (bf16[176,2048]{1,0:T(8,128)(2,1)}, bf16[176,2048]{1,0:T(8,128)(2,1)S(1)}, u32[]{:S(2)}) copy-start(bf16[176,2048]{1,0:T(8,128)(2,1)S(1)} %collective-permute-done.6.refs_7_) | copy-start | bytes 2162692
  152.1 26.0 %collective-permute-start.7 = (bf16[176,2048]{1,0:T(8,128)(2,1)S(1)}, bf16[176,2048]{1,0:T(8,128)(2,1)S(1)}, u32[]{:S(2)}, u32[]{:S(2)}) collective-permute-start(bf16[176,2048]{1,0:T(8,128)(2,1)S(1)} %collective-permute-done.3.refs_4_), channel_id=1, source_target_pairs={{0,4},{4,0},{8,12},{12,8},{16,20},{20,16},{24,28},{28,24},{32,36},... | collective-permute-start | bytes 2162696 | tf_op jit(solution)/shard_map/ppermute | solution.py:291
  173.8 7.6 %collective-permute-start.10 = (bf16[176,2048]{1,0:T(8,128)(2,1)S(1)}, bf16[176,2048]{1,0:T(8,128)(2,1)S(1)}, u32[]{:S(2)}, u32[]{:S(2)}) collective-permute-start(bf16[176,2048]{1,0:T(8,128)(2,1)S(1)} %collective-permute-done.6.refs_7_), channel_id=1, source_target_pairs={{0,4},{4,0},{8,12},{12,8},{16,20},{20,16},{24,28},{28,24},{32,36},... | collective-permute-start | bytes 2162696 | tf_op jit(solution)/shard_map/ppermute | solution.py:291
  175.7 6.8 %collective-permute-start.8 = (bf16[176,2048]{1,0:T(8,128)(2,1)S(1)}, bf16[176,2048]{1,0:T(8,128)(2,1)S(1)}, u32[]{:S(2)}, u32[]{:S(2)}) collective-permute-start(bf16[176,2048]{1,0:T(8,128)(2,1)S(1)} %collective-permute-done.4.refs_5_), channel_id=1, source_target_pairs={{0,4},{4,0},{8,12},{12,8},{16,20},{20,16},{24,28},{28,24},{32,36},... | collective-permute-start | bytes 2162696 | tf_op jit(solution)/shard_map/ppermute | solution.py:291
  178.2 6.1 %collective-permute-start.9 = (bf16[176,2048]{1,0:T(8,128)(2,1)S(1)}, bf16[176,2048]{1,0:T(8,128)(2,1)}, u32[]{:S(2)}, u32[]{:S(2)}) collective-permute-start(bf16[176,2048]{1,0:T(8,128)(2,1)S(1)} %collective-permute-done.5.refs_6_), channel_id=1, source_target_pairs={{0,4},{4,0},{8,12},{12,8},{16,20},{20,16},{24,28},{28,24},{32,36},... | collective-permute-start | bytes 2162696 | tf_op jit(solution)/shard_map/ppermute | solution.py:291
  197.2 56.4 %all-to-all-start.3 = ((bf16[32,192,128]{2,1,0:T(8,128)(2,1)}), bf16[32,192,128]{2,1,0:T(8,128)(2,1)S(1)}, u32[]{:S(2)}, u32[]{:S(2)}) async-start(bf16[32,192,128]{2,1,0:T(8,128)(2,1)} %bitcast.39), calls=%async_computation.3 | async-start | bytes 3145728 | tf_op jit(solution)/shard_map/all_to_all | solution.py:301
  (8 other events, 36.3 us)

commit v2 on v1

--- a/solution.py
+++ b/solution.py
@@ -16,7 +16,7 @@
 GROUP = HEADS // KV
 WIDTH = HEADS * HEAD
 UNITS = 352
-PADDED = 768
+PADDED = 1536
 PIECE = 176
 PITCH = 17
 CHUNK = 96
@@ -172,43 +172,47 @@
     pltpu.make_async_copy(down_ref.at[rows, :], piece_ref, sem).wait()
 
 
-def expert_kernel(plane_ref, recv_ref, *refs):
-    sources, rest = refs[:12], refs[12:]
-    out_ref, tiles_ref, rows_ref, x_ref, held_ref, hidden_ref, sems, tile_sems = rest
+def assemble_kernel(plane_ref, *refs):
+    sources, (held_ref, sems) = refs[:12], refs[12:]
     plane = plane_ref[0]
-    up_ref = held_ref.at[pl.ds(0, QUART * UNITS), :]
-    down_ref = held_ref.at[pl.ds(QUART * UNITS, 2 * PADDED), :]
-    down_at = QUART * UNITS
-    arrivals = []
-    for n in range(SLOTS // CHUNK):
-        some = pl.ds(n * CHUNK, CHUNK)
-        arrivals.append(
-            pltpu.make_async_copy(recv_ref.at[some], tiles_ref.at[some], tile_sems.at[n])
-        )
-        arrivals[n].start()
     copies = []
-    for n, at in enumerate((0, down_at, UNITS, down_at + UNITS)):
+    for n, at in enumerate((0, PADDED, UNITS, PADDED + UNITS)):
         copies.append(
             pltpu.make_async_copy(sources[n], held_ref.at[pl.ds(at, UNITS), :], sems.at[n])
         )
     for n in range(8):
         shard, step = n // 4, n % 4
         quarter = lax.rem(plane - step + 4, 4)
-        at = jnp.where(
-            quarter < 2,
-            (2 + shard) * UNITS + quarter * PIECE,
-            down_at + PADDED + shard * UNITS + (quarter - 2) * PIECE,
-        )
+        at = (2 + shard) * UNITS + lax.rem(quarter, 2) * PIECE
+        at = at + jnp.where(quarter < 2, 0, PADDED)
         place = pl.ds(pl.multiple_of(at, PIECE // 11), PIECE)
         copies.append(
             pltpu.make_async_copy(sources[4 + n], held_ref.at[place, :], sems.at[4 + n])
         )
-    for n in (0, 2, 1, 3, 4, 5, 6, 7, 8, 9, 10, 11):
-        copies[n].start()
-    for half in range(2):
-        end = (half + 1) * PADDED
-        down_ref[end - 64 : end, :] = jnp.zeros((64, WIDTH), BF16)
-        hidden_ref[:, end - 128 : end] = jnp.zeros((SLOTS, 128), BF16)
+    for one in copies:
+        one.start()
+    empty = jnp.zeros((PADDED - QUART * UNITS, WIDTH), BF16)
+    for end in (PADDED, 2 * PADDED):
+        held_ref[end - PADDED + QUART * UNITS : end, :] = empty
+    for one in copies:
+        one.wait()
+
+
+def expert_kernel(
+    recv_ref, weight_ref, out_ref, tiles_ref, rows_ref, x_ref, held_ref, hidden_ref, sems, weight_sems
+):
+    arrivals = []
+    for n in range(SLOTS // CHUNK):
+        some = pl.ds(n * CHUNK, CHUNK)
+        arrivals.append(pltpu.make_async_copy(recv_ref.at[some], tiles_ref.at[some], sems.at[n]))
+    parts = []
+    for n, (at, size) in enumerate(((0, 512), (512, 1024), (1536, 1536))):
+        some = pl.ds(at, size)
+        parts.append(
+            pltpu.make_async_copy(weight_ref.at[some, :], held_ref.at[some, :], weight_sems.at[n])
+        )
+    for one in arrivals + parts:
+        one.start()
 
     def unpack(t, carry):
         rows_ref[pl.ds(t * PITCH, HEADS), :] = tiles_ref[t].astype(F32)
@@ -221,19 +225,17 @@
         x_ref[:, j * HEAD : (j + 1) * HEAD] = rows_ref[
             pl.ds(j, SLOTS, stride=PITCH), :
         ].astype(BF16)
-    for half in range(2):
-        for n in ((0, 2), (1, 3, 4, 5, 6, 7, 8, 9, 10, 11))[half]:
-            copies[n].wait()
-        for start, size in ((0, 256), (256, 256), (512, 192)):
-            at = half * 2 * UNITS + start
-            hidden = 0.5 * dot(x_ref[...], up_ref[at : at + size, :], 1, 1)
-            hidden = hidden + hidden * jnp.tanh(hidden)
-            at = half * PADDED + start
-            hidden_ref[:, at : at + size] = hidden.astype(BF16)
+    for part, blocks in ((0, (0, 1)), (1, (2, 3, 4, 5))):
+        parts[part].wait()
+        for n in blocks:
+            here = slice(n * 256, (n + 1) * 256)
+            hidden = 0.5 * dot(x_ref[...], held_ref[here, :], 1, 1)
+            hidden_ref[:, here] = (hidden + hidden * jnp.tanh(hidden)).astype(BF16)
+    parts[2].wait()
 
     def columns(n, carry):
         here = pl.ds(pl.multiple_of(n * 256, 256), 256)
-        result = dot(hidden_ref[...], down_ref[:, here])
+        result = dot(hidden_ref[...], held_ref[PADDED:, here])
         rows_ref[pl.ds(2 * n, SLOTS, stride=PITCH), :] = result[:, :HEAD]
         rows_ref[pl.ds(2 * n + 1, SLOTS, stride=PITCH), :] = result[:, HEAD:]
         return carry
@@ -248,7 +250,7 @@
     for n in range(SLOTS // CHUNK):
         lax.fori_loop(n * CHUNK, (n + 1) * CHUNK, pack, 0, unroll=16)
         some = pl.ds(n * CHUNK, CHUNK)
-        leaving.append(pltpu.make_async_copy(tiles_ref.at[some], out_ref.at[some], tile_sems.at[n]))
+        leaving.append(pltpu.make_async_copy(tiles_ref.at[some], out_ref.at[some], sems.at[n]))
         leaving[n].start()
     for one in leaving:
         one.wait()
@@ -364,25 +366,33 @@
     )(slots, queries, before, decay_logarithm, lin_gain.reshape(1, WIDTH), window, inner)
 
     received = routed(send)
+    held = call(
+        assemble_kernel,
+        [((2 * PADDED, WIDTH), BF16)],
+        [SMEM] + [FAR] * 12,
+        [pltpu.SemaphoreType.DMA((12,))],
+        room=62,
+        moved=24_000_000,
+    )(plane, up, w_down, up_c, down_c, *pieces, *onward)
     computed = call(
         expert_kernel,
         [((SLOTS, HEADS, HEAD), BF16)],
-        [SMEM] + [FAR] * 13,
+        [FAR] * 2,
         [
             pltpu.VMEM((SLOTS, HEADS, HEAD), BF16),
             pltpu.VMEM((SLOTS * PITCH, HEAD), F32),
             pltpu.VMEM((SLOTS, WIDTH), BF16),
-            pltpu.VMEM((QUART * UNITS + 2 * PADDED, WIDTH), BF16),
-            pltpu.VMEM((SLOTS, 2 * PADDED), BF16),
-            pltpu.SemaphoreType.DMA((12,)),
+            pltpu.VMEM((2 * PADDED, WIDTH), BF16),
+            pltpu.VMEM((SLOTS, PADDED), BF16),
             pltpu.SemaphoreType.DMA((SLOTS // CHUNK,)),
+            pltpu.SemaphoreType.DMA((3,)),
         ],
         room=62,
         place=FAR,
         flops=4_500_000_000,
         moved=15_000_000,
         exps=1 << 19,
-    )(plane, received, up, w_down, up_c, down_c, *pieces, *onward)
+    )(received, held)
     back = routed(computed)
     return call(
         combine_kernel,

time: 256 us -> 264 us (1.031)
  Pallas kernels: 32.3 us -> 39.1 us
    pallas_call x1 -> x2, Pallas kernels: 12.9 us -> 19.7 us  [the longest x1 10.8 us: per_device(): call(expert_kernel, [((SLOTS, HEADS, HEAD), BF16)], [FAR] * 2, [pltpu.VME...]
  transfers between devices with their start and end apart: 15 -> 15, of which waited for: 6 -> 6; matrix products, arithmetic and copies ran while one was open for 1% -> 1% of each run, Pallas kernels for 4% -> 7%
where the time goes in v2:
time: 264 us; the launch traced here: 263 us
  waiting for transfers between devices  135 us (51%)
  starting transfers between devices  82.1 us (31%)
  Pallas kernels  39.1 us (15%)
  local copies, waits for them, and re-layouts  5.46 us (2%)
    ppermute x7, waiting for transfers between devices, swapped(): return lax.ppermute(x, 'wide', [(i, i ^ bit) for i in range(peers)])  47.4 us
    all_to_all x2, waiting for transfers between devices, routed(): lax.all_to_all(flat, 'wide', split_axis=0, concat_axis=0, tiled=True, axi...  43.8 us
    all_to_all x2, starting transfers between devices, exchanged(): return lax.all_to_all(x, axis, split_axis=0, concat_axis=0, tiled=True)  32.9 us
    ppermute x3, waiting for transfers between devices, per_device(): pieces.append(lax.ppermute(pieces[0], 'narrow', around))  26.9 us
    all_to_all x2, starting transfers between devices, routed(): lax.all_to_all(flat, 'wide', split_axis=0, concat_axis=0, tiled=True, axi...  20.8 us
    all_to_all x2, waiting for transfers between devices, exchanged(): return lax.all_to_all(x, axis, split_axis=0, concat_axis=0, tiled=True)  16.8 us
    ppermute x7, starting transfers between devices, swapped(): return lax.ppermute(x, 'wide', [(i, i ^ bit) for i in range(peers)])  15.4 us
    pallas_call x1, Pallas kernels, per_device(): call(expert_kernel, [((SLOTS, HEADS, HEAD), BF16)], [FAR] * 2, [pltpu.VME...  10.8 us
  transfers between devices with their start and end apart: 15, of which 6 were waited for; matrix products, arithmetic and copies ran while one was open for 1% of the time, Pallas kernels for 7%

profile of v2, /device:TPU:48, one launch (start us, length us, event | category | flops | bytes accessed | tf_op | source)
XLA Modules:
  0.0 262.8 jit_solution(14669213169262012864)
XLA Ops:
  0.0 2.6 shard_map.91
  2.6 20.8 %all-to-all-start = ((f32[512,1,128]{2,1,0:T(1,128)}), f32[512,1,128]{2,1,0:T(1,128)S(1)}, u32[]{:S(2)}, u32[]{:S(2)}) async-start(f32[512,1,128]{2,1,0:T(1,128)} %bitcast.43), calls=%async_computation | async-start | bytes 524288 | tf_op jit(solution)/shard_map/all_to_all | solution.py:297
  23.4 3.4 %collective-permute-start = (bf16[256,256]{1,0:T(8,128)(2,1)}, bf16[256,256]{1,0:T(8,128)(2,1)S(1)}, u32[]{:S(2)}, u32[]{:S(2)}) collective-permute-start(bf16[256,256]{1,0:T(8,128)(2,1)} %get-tuple-element.12), channel_id=1, source_target_pairs={{0,1},{1,2},{2,3},{3,4},{4,5},{5,6},{6,7},{7,8},{8,9},{9,10},{10,1... | collective-permute-start | bytes 393224 | tf_op jit(solution)/shard_map/ppermute | solution.py:322
  27.7 9.7 %all-to-all-done = f32[512,1,128]{2,1,0:T(1,128)S(1)} async-done(((f32[512,1,128]{2,1,0:T(1,128)}), f32[512,1,128]{2,1,0:T(1,128)S(1)}, u32[]{:S(2)}, u32[]{:S(2)}) %all-to-all-start) | async-done | bytes 262176 | tf_op jit(solution)/shard_map/all_to_all | solution.py:297
  38.9 12.1 %all-to-all-start.1 = ((f32[512,1,128]{2,1,0:T(1,128)}), f32[512,1,128]{2,1,0:T(1,128)S(1)}, u32[]{:S(2)}, u32[]{:S(2)}) async-start(f32[512,1,128]{2,1,0:T(1,128)} %bitcast.5), calls=%async_computation.1 | async-start | bytes 524288 | tf_op jit(solution)/shard_map/all_to_all | solution.py:297
  52.2 5.6 %shard_map.93 = (f32[128,2048]{1,0:T(8,128)S(1)}, f32[128,2048]{1,0:T(8,128)S(1)}) custom-call(s32[1]{0:T(128)} %bitcast.8.started_ref, bf16[128,2048]{1,0:T(8,128)(2,1)S(1)} %copy-done, bf16[128,256]{1,0:T(8,128)(2,1)S(1)} %copy-done.1, bf16[128,256]{1,0:T(8,128)(2,1)S(1)} %copy-done.2, bf16[256,256]{1,0:T(8,128)(2,1)S(1)} %collective-permute-done.prev_ref, ...), custom_call_target="tpu_custom_call" | custom-call | flops 536870912 | bytes 3000000 | tf_op jit(solution)/shard_map/pallas_call | solution.py:351
  57.8 7.1 %all-to-all-done.1 = f32[512,1,128]{2,1,0:T(1,128)S(1)} async-done(((f32[512,1,128]{2,1,0:T(1,128)}), f32[512,1,128]{2,1,0:T(1,128)S(1)}, u32[]{:S(2)}, u32[]{:S(2)}) %all-to-all-start.1) | async-done | bytes 262176 | tf_op jit(solution)/shard_map/all_to_all | solution.py:297
  64.9 5.7 %shard_map.94 = (bf16[128,16,128]{2,1,0:T(8,128)(2,1)S(1)}, bf16[384,16,128]{2,1,0:T(8,128)(2,1)}) custom-call(s32[256]{0:T(256)S(1)} %multiply_add_fusion.slot_ref, bf16[128,2048]{1,0:T(8,128)(2,1)S(1)} %copy-done, f32[512,128]{1,0:T(8,128)S(1)} %bitcast.36, f32[2,128]{1,0:T(2,128)S(1)} %copy-done.4, f32[1,2048]{1,0:T(1,128)S(1)} %bitcast.38, ...), custom_call_target="tpu_custom_call" | custom-call | flops 268435456 | bytes 5000000 | tf_op jit(solution)/shard_map/pallas_call | solution.py:359
  70.6 8.1 %all-to-all-start.2 = ((bf16[32,192,128]{2,1,0:T(8,128)(2,1)}), bf16[32,192,128]{2,1,0:T(8,128)(2,1)}, u32[]{:S(2)}, u32[]{:S(2)}) async-start(bf16[32,192,128]{2,1,0:T(8,128)(2,1)} %bitcast.9), calls=%async_computation.2 | async-start | bytes 3145728 | tf_op jit(solution)/shard_map/all_to_all | solution.py:303
  78.7 2.1 shard_map.95
  80.9 3.0 %collective-permute-start.3 = (bf16[176,2048]{1,0:T(8,128)(2,1)}, bf16[176,2048]{1,0:T(8,128)(2,1)S(1)}, u32[]{:S(2)}, u32[]{:S(2)}) collective-permute-start(bf16[176,2048]{1,0:T(8,128)(2,1)} %shard_map.95), channel_id=1, source_target_pairs={{0,8},{4,12},{8,0},{12,4},{16,24},{20,28},{24,16},{28,20},{32,40},... | collective-permute-start | bytes 2162696 | tf_op jit(solution)/shard_map/ppermute | solution.py:293
  83.9 47.4 %collective-permute-done.3.refs_4_ = bf16[176,2048]{1,0:T(8,128)(2,1)S(1)} collective-permute-done((bf16[176,2048]{1,0:T(8,128)(2,1)}, bf16[176,2048]{1,0:T(8,128)(2,1)S(1)}, u32[]{:S(2)}, u32[]{:S(2)}) %collective-permute-start.3) | collective-permute-done | bytes 720928 | tf_op jit(solution)/shard_map/ppermute | solution.py:293
  131.3 3.6 %collective-permute-start.6 = (bf16[176,2048]{1,0:T(8,128)(2,1)S(1)}, bf16[176,2048]{1,0:T(8,128)(2,1)S(1)}, u32[]{:S(2)}, u32[]{:S(2)}) collective-permute-start(bf16[176,2048]{1,0:T(8,128)(2,1)S(1)} %collective-permute-done.3.refs_4_), channel_id=1, source_target_pairs={{0,3},{1,0},{2,1},{3,2},{4,7},{5,4},{6,5},{7,6},{8,11},{9,8},{10,9... | collective-permute-start | bytes 2162696 | tf_op jit(solution)/shard_map/ppermute | solution.py:337
  136.8 2.3 collective-permute-start.4
  139.1 2.1 collective-permute-start.2
  141.2 3.9 %collective-permute-start.5 = (bf16[176,2048]{1,0:T(8,128)(2,1)S(1)}, bf16[176,2048]{1,0:T(8,128)(2,1)S(1)}, u32[]{:S(2)}, u32[]{:S(2)}) collective-permute-start(bf16[176,2048]{1,0:T(8,128)(2,1)S(1)} %collective-permute-done.3.refs_4_), channel_id=1, source_target_pairs={{0,2},{1,3},{2,0},{3,1},{4,6},{5,7},{6,4},{7,5},{8,10},{9,11},{10,... | collective-permute-start | bytes 2162696 | tf_op jit(solution)/shard_map/ppermute | solution.py:337
  145.1 7.1 %collective-permute-done.6.refs_7_ = bf16[176,2048]{1,0:T(8,128)(2,1)S(1)} collective-permute-done((bf16[176,2048]{1,0:T(8,128)(2,1)S(1)}, bf16[176,2048]{1,0:T(8,128)(2,1)S(1)}, u32[]{:S(2)}, u32[]{:S(2)}) %collective-permute-start.6) | collective-permute-done | bytes 720928 | tf_op jit(solution)/shard_map/ppermute | solution.py:337
  154.1 19.8 %collective-permute-done.4.refs_5_ = bf16[176,2048]{1,0:T(8,128)(2,1)S(1)} collective-permute-done((bf16[176,2048]{1,0:T(8,128)(2,1)S(1)}, bf16[176,2048]{1,0:T(8,128)(2,1)S(1)}, u32[]{:S(2)}, u32[]{:S(2)}) %collective-permute-start.4) | collective-permute-done | bytes 720928 | tf_op jit(solution)/shard_map/ppermute | solution.py:337
  175.9 2.4 collective-permute-start.8
  178.3 2.1 collective-permute-start.9
  184.4 8.9 %shard_map.96.weight_ref = bf16[3072,2048]{1,0:T(8,128)(2,1)} custom-call(s32[1]{0:T(128)} %bitcast.11.plane_ref, bf16[352,2048]{1,0:T(8,128)(2,1)} %bitcast.40, bf16[352,2048]{1,0:T(8,128)(2,1)} %refs_1_.1, bf16[352,2048]{1,0:T(8,128)(2,1)} %copy-done.7, bf16[352,2048]{1,0:T(8,128)(2,1)} %copy-done.8, bf16[176,2048]{1,0:T(8,128)(2,1)} %copy-done.9, ...), custom_call_target="tpu_custom_call" | custom-call | bytes 24000000 | tf_op jit(solution)/shard_map/pallas_call | solution.py:369
  193.3 10.8 %shard_map.97 = bf16[384,16,128]{2,1,0:T(8,128)(2,1)} custom-call(bf16[384,16,128]{2,1,0:T(8,128)(2,1)} %bitcast.10.recv_ref, bf16[3072,2048]{1,0:T(8,128)(2,1)} %shard_map.96.weight_ref), custom_call_target="tpu_custom_call" | custom-call | flops 4499999744 | bytes 15000000 | tf_op jit(solution)/shard_map/pallas_call | solution.py:377
  204.1 12.7 %all-to-all-start.3 = ((bf16[32,192,128]{2,1,0:T(8,128)(2,1)}), bf16[32,192,128]{2,1,0:T(8,128)(2,1)S(1)}, u32[]{:S(2)}, u32[]{:S(2)}) async-start(bf16[32,192,128]{2,1,0:T(8,128)(2,1)} %bitcast.42), calls=%async_computation.3 | async-start | bytes 3145728 | tf_op jit(solution)/shard_map/all_to_all | solution.py:303
  217.0 43.8 %all-to-all-done.3 = bf16[32,192,128]{2,1,0:T(8,128)(2,1)S(1)} async-done(((bf16[32,192,128]{2,1,0:T(8,128)(2,1)}), bf16[32,192,128]{2,1,0:T(8,128)(2,1)S(1)}, u32[]{:S(2)}, u32[]{:S(2)}) %all-to-all-start.3) | async-done | bytes 1572896 | tf_op jit(solution)/shard_map/all_to_all | solution.py:303
  (60 shorter events, 15.4 us)
Async XLA Ops:
  0.0 52.1 %copy-start.1 = (bf16[128,256]{1,0:T(8,128)(2,1)S(1)}, bf16[128,256]{1,0:T(8,128)(2,1)}, u32[]{:S(2)}) copy-start(bf16[128,256]{1,0:T(8,128)(2,1)} %key_ref.3) | copy-start | bytes 196612
  0.0 52.1 %copy-start.2 = (bf16[128,256]{1,0:T(8,128)(2,1)S(1)}, bf16[128,256]{1,0:T(8,128)(2,1)}, u32[]{:S(2)}) copy-start(bf16[128,256]{1,0:T(8,128)(2,1)} %value_ref.3) | copy-start | bytes 196612
  0.0 52.2 %copy-start.4 = (f32[2,128]{1,0:T(2,128)S(1)}, f32[2,128]{1,0:T(2,128)}, u32[]{:S(2)}) copy-start(f32[2,128]{1,0:T(2,128)} %decay_ref.5) | copy-start | bytes 3076
  0.0 52.2 %copy-start = (bf16[128,2048]{1,0:T(8,128)(2,1)S(1)}, bf16[128,2048]{1,0:T(8,128)(2,1)}, u32[]{:S(2)}) copy-start(bf16[128,2048]{1,0:T(8,128)(2,1)} %query_ref.3) | copy-start | bytes 1572868
  2.6 34.8 %all-to-all-start = ((f32[512,1,128]{2,1,0:T(1,128)}), f32[512,1,128]{2,1,0:T(1,128)S(1)}, u32[]{:S(2)}, u32[]{:S(2)}) async-start(f32[512,1,128]{2,1,0:T(1,128)} %bitcast.43), calls=%async_computation | async-start | bytes 524288 | tf_op jit(solution)/shard_map/all_to_all | solution.py:297
  23.4 28.7 %collective-permute-start = (bf16[256,256]{1,0:T(8,128)(2,1)}, bf16[256,256]{1,0:T(8,128)(2,1)S(1)}, u32[]{:S(2)}, u32[]{:S(2)}) collective-permute-start(bf16[256,256]{1,0:T(8,128)(2,1)} %get-tuple-element.12), channel_id=1, source_target_pairs={{0,1},{1,2},{2,3},{3,4},{4,5},{5,6},{6,7},{7,8},{8,9},{9,10},{10,1... | collective-permute-start | bytes 393224 | tf_op jit(solution)/shard_map/ppermute | solution.py:322
  37.5 27.5 %copy-start.3 = (f32[2048]{0:T(1024)S(1)}, f32[2048]{0:T(1024)}, u32[]{:S(2)}) copy-start(f32[2048]{0:T(1024)} %param.13) | copy-start | bytes 24580
  38.9 26.0 %all-to-all-start.1 = ((f32[512,1,128]{2,1,0:T(1,128)}), f32[512,1,128]{2,1,0:T(1,128)S(1)}, u32[]{:S(2)}, u32[]{:S(2)}) async-start(f32[512,1,128]{2,1,0:T(1,128)} %bitcast.5), calls=%async_computation.1 | async-start | bytes 524288 | tf_op jit(solution)/shard_map/all_to_all | solution.py:297
  70.6 122.7 %all-to-all-start.2 = ((bf16[32,192,128]{2,1,0:T(8,128)(2,1)}), bf16[32,192,128]{2,1,0:T(8,128)(2,1)}, u32[]{:S(2)}, u32[]{:S(2)}) async-start(bf16[32,192,128]{2,1,0:T(8,128)(2,1)} %bitcast.9), calls=%async_computation.2 | async-start | bytes 3145728 | tf_op jit(solution)/shard_map/all_to_all | solution.py:303
  78.7 56.2 %copy-start.5 = (bf16[2048,352]{0,1:T(8,128)(2,1)S(1)}, bf16[2048,352]{0,1:T(8,128)(2,1)}, u32[]{:S(2)}) copy-start(bf16[2048,352]{0,1:T(8,128)(2,1)} %param.16) | copy-start | bytes 4325380
  78.7 60.4 %copy-start.6 = (bf16[352,2048]{1,0:T(8,128)(2,1)S(1)}, bf16[352,2048]{1,0:T(8,128)(2,1)}, u32[]{:S(2)}) copy-start(bf16[352,2048]{1,0:T(8,128)(2,1)} %refs_1_.1) | copy-start | bytes 4325380
  80.9 50.4 %collective-permute-start.3 = (bf16[176,2048]{1,0:T(8,128)(2,1)}, bf16[176,2048]{1,0:T(8,128)(2,1)S(1)}, u32[]{:S(2)}, u32[]{:S(2)}) collective-permute-start(bf16[176,2048]{1,0:T(8,128)(2,1)} %shard_map.95), channel_id=1, source_target_pairs={{0,8},{4,12},{8,0},{12,4},{16,24},{20,28},{24,16},{28,20},{32,40},... | collective-permute-start | bytes 2162696 | tf_op jit(solution)/shard_map/ppermute | solution.py:293
  131.3 53.1 %copy-start.9 = (bf16[176,2048]{1,0:T(8,128)(2,1)}, bf16[176,2048]{1,0:T(8,128)(2,1)S(1)}, u32[]{:S(2)}) copy-start(bf16[176,2048]{1,0:T(8,128)(2,1)S(1)} %collective-permute-done.3.refs_4_) | copy-start | bytes 2162692
  131.3 20.9 %collective-permute-start.6 = (bf16[176,2048]{1,0:T(8,128)(2,1)S(1)}, bf16[176,2048]{1,0:T(8,128)(2,1)S(1)}, u32[]{:S(2)}, u32[]{:S(2)}) collective-permute-start(bf16[176,2048]{1,0:T(8,128)(2,1)S(1)} %collective-permute-done.3.refs_4_), channel_id=1, source_target_pairs={{0,3},{1,0},{2,1},{3,2},{4,7},{5,4},{6,5},{7,6},{8,11},{9,8},{10,9... | collective-permute-start | bytes 2162696 | tf_op jit(solution)/shard_map/ppermute | solution.py:337
  134.9 45.5 %collective-permute-start.1 = (bf16[352,2048]{1,0:T(8,128)(2,1)S(1)}, bf16[352,2048]{1,0:T(8,128)(2,1)S(1)}, u32[]{:S(2)}, u32[]{:S(2)}) collective-permute-start(bf16[352,2048]{1,0:T(8,128)(2,1)S(1)} %bitcast.41), channel_id=1, source_target_pairs={{0,4},{4,0},{8,12},{12,8},{16,20},{20,16},{24,28},{28,24},{32,36},... | collective-permute-start | bytes 4325384 | tf_op jit(solution)/shard_map/ppermute | solution.py:293
  136.8 37.1 %collective-permute-start.4 = (bf16[176,2048]{1,0:T(8,128)(2,1)S(1)}, bf16[176,2048]{1,0:T(8,128)(2,1)S(1)}, u32[]{:S(2)}, u32[]{:S(2)}) collective-permute-start(bf16[176,2048]{1,0:T(8,128)(2,1)S(1)} %collective-permute-done.3.refs_4_), channel_id=1, source_target_pairs={{0,1},{1,2},{2,3},{3,0},{4,5},{5,6},{6,7},{7,4},{8,9},{9,10},{10,1... | collective-permute-start | bytes 2162696 | tf_op jit(solution)/shard_map/ppermute | solution.py:337
  139.1 41.3 %collective-permute-start.2 = (bf16[352,2048]{1,0:T(8,128)(2,1)S(1)}, bf16[352,2048]{1,0:T(8,128)(2,1)S(1)}, u32[]{:S(2)}, u32[]{:S(2)}) collective-permute-start(bf16[352,2048]{1,0:T(8,128)(2,1)S(1)} %copy-done.6), channel_id=1, source_target_pairs={{0,4},{4,0},{8,12},{12,8},{16,20},{20,16},{24,28},{28,24},{32,36},... | collective-permute-start | bytes 4325384 | tf_op jit(solution)/shard_map/ppermute | solution.py:293
  141.2 34.6 %collective-permute-start.5 = (bf16[176,2048]{1,0:T(8,128)(2,1)S(1)}, bf16[176,2048]{1,0:T(8,128)(2,1)S(1)}, u32[]{:S(2)}, u32[]{:S(2)}) collective-permute-start(bf16[176,2048]{1,0:T(8,128)(2,1)S(1)} %collective-permute-done.3.refs_4_), channel_id=1, source_target_pairs={{0,2},{1,3},{2,0},{3,1},{4,6},{5,7},{6,4},{7,5},{8,10},{9,11},{10,... | collective-permute-start | bytes 2162696 | tf_op jit(solution)/shard_map/ppermute | solution.py:337
  152.2 30.5 %copy-start.10 = (bf16[176,2048]{1,0:T(8,128)(2,1)}, bf16[176,2048]{1,0:T(8,128)(2,1)S(1)}, u32[]{:S(2)}) copy-start(bf16[176,2048]{1,0:T(8,128)(2,1)S(1)} %collective-permute-done.6.refs_7_) | copy-start | bytes 2162692
  152.2 26.1 %collective-permute-start.7 = (bf16[176,2048]{1,0:T(8,128)(2,1)S(1)}, bf16[176,2048]{1,0:T(8,128)(2,1)S(1)}, u32[]{:S(2)}, u32[]{:S(2)}) collective-permute-start(bf16[176,2048]{1,0:T(8,128)(2,1)S(1)} %collective-permute-done.3.refs_4_), channel_id=1, source_target_pairs={{0,4},{4,0},{8,12},{12,8},{16,20},{20,16},{24,28},{28,24},{32,36},... | collective-permute-start | bytes 2162696 | tf_op jit(solution)/shard_map/ppermute | solution.py:293
  173.9 7.6 %collective-permute-start.10 = (bf16[176,2048]{1,0:T(8,128)(2,1)S(1)}, bf16[176,2048]{1,0:T(8,128)(2,1)S(1)}, u32[]{:S(2)}, u32[]{:S(2)}) collective-permute-start(bf16[176,2048]{1,0:T(8,128)(2,1)S(1)} %collective-permute-done.6.refs_7_), channel_id=1, source_target_pairs={{0,4},{4,0},{8,12},{12,8},{16,20},{20,16},{24,28},{28,24},{32,36},... | collective-permute-start | bytes 2162696 | tf_op jit(solution)/shard_map/ppermute | solution.py:293
  175.9 6.8 %collective-permute-start.8 = (bf16[176,2048]{1,0:T(8,128)(2,1)S(1)}, bf16[176,2048]{1,0:T(8,128)(2,1)S(1)}, u32[]{:S(2)}, u32[]{:S(2)}) collective-permute-start(bf16[176,2048]{1,0:T(8,128)(2,1)S(1)} %collective-permute-done.4.refs_5_), channel_id=1, source_target_pairs={{0,4},{4,0},{8,12},{12,8},{16,20},{20,16},{24,28},{28,24},{32,36},... | collective-permute-start | bytes 2162696 | tf_op jit(solution)/shard_map/ppermute | solution.py:293
  178.3 6.1 %collective-permute-start.9 = (bf16[176,2048]{1,0:T(8,128)(2,1)S(1)}, bf16[176,2048]{1,0:T(8,128)(2,1)}, u32[]{:S(2)}, u32[]{:S(2)}) collective-permute-start(bf16[176,2048]{1,0:T(8,128)(2,1)S(1)} %collective-permute-done.5.refs_6_), channel_id=1, source_target_pairs={{0,4},{4,0},{8,12},{12,8},{16,20},{20,16},{24,28},{28,24},{32,36},... | collective-permute-start | bytes 2162696 | tf_op jit(solution)/shard_map/ppermute | solution.py:293
  204.1 56.8 %all-to-all-start.3 = ((bf16[32,192,128]{2,1,0:T(8,128)(2,1)}), bf16[32,192,128]{2,1,0:T(8,128)(2,1)S(1)}, u32[]{:S(2)}, u32[]{:S(2)}) async-start(bf16[32,192,128]{2,1,0:T(8,128)(2,1)} %bitcast.42), calls=%async_computation.3 | async-start | bytes 3145728 | tf_op jit(solution)/shard_map/all_to_all | solution.py:303
  (8 other events, 36.6 us)

commit v3 on v2

--- a/solution.py
+++ b/solution.py
@@ -118,7 +118,7 @@
             window_ref[:, here] = dot(both.astype(BF16), values)
             return carry
 
-        lax.fori_loop(0, GROUP, one, 0, unroll=2)
+        lax.fori_loop(0, GROUP, one, 0, unroll=8)
 
 
 def finish_kernel(
@@ -145,7 +145,7 @@
             rows_ref[pl.ds(number, TOK, stride=PITCH), :] = normed + window_ref[:, here]
             return carry
 
-        lax.fori_loop(0, GROUP, one, 0, unroll=2)
+        lax.fori_loop(0, GROUP, one, 0, unroll=8)
 
     def place(t, carry):
         row = rows_ref[pl.ds(t * PITCH, HEADS), :].astype(BF16)
@@ -154,7 +154,7 @@
         send_ref[slot_ref[2 * t + 1]] = row
         return carry
 
-    lax.fori_loop(0, TOK, place, 0, unroll=8)
+    lax.fori_loop(0, TOK, place, 0, unroll=16)
 
 
 def pick_kernel(plane_ref, up_ref, down_ref, piece_ref, sem):

time: 264 us -> 260 us (0.985)
  Pallas kernels: 39.1 us -> 34.7 us
  transfers between devices with their start and end apart: 15 -> 15, of which waited for: 6 -> 6; matrix products, arithmetic and copies ran while one was open for 1% -> 1% of each run, Pallas kernels for 7% -> 6%
where the time goes in v3:
time: 260 us; the launch traced here: 259 us
  waiting for transfers between devices  136 us (52%)
  starting transfers between devices  81.5 us (31%)
  Pallas kernels  34.7 us (13%)
  local copies, waits for them, and re-layouts  5.46 us (2%)
    ppermute x7, waiting for transfers between devices, swapped(): return lax.ppermute(x, 'wide', [(i, i ^ bit) for i in range(peers)])  47.3 us
    all_to_all x2, waiting for transfers between devices, routed(): lax.all_to_all(flat, 'wide', split_axis=0, concat_axis=0, tiled=True, axi...  43.7 us
    all_to_all x2, starting transfers between devices, exchanged(): return lax.all_to_all(x, axis, split_axis=0, concat_axis=0, tiled=True)  32.9 us
    ppermute x3, waiting for transfers between devices, per_device(): pieces.append(lax.ppermute(pieces[0], 'narrow', around))  26.6 us
    all_to_all x2, starting transfers between devices, routed(): lax.all_to_all(flat, 'wide', split_axis=0, concat_axis=0, tiled=True, axi...  20 us
    all_to_all x2, waiting for transfers between devices, exchanged(): return lax.all_to_all(x, axis, split_axis=0, concat_axis=0, tiled=True)  18.8 us
    ppermute x7, starting transfers between devices, swapped(): return lax.ppermute(x, 'wide', [(i, i ^ bit) for i in range(peers)])  15.4 us
    pallas_call x1, Pallas kernels, per_device(): call(expert_kernel, [((SLOTS, HEADS, HEAD), BF16)], [FAR] * 2, [pltpu.VME...  10.8 us
  transfers between devices with their start and end apart: 15, of which 6 were waited for; matrix products, arithmetic and copies ran while one was open for 1% of the time, Pallas kernels for 6%

profile of v3, /device:TPU:48, one launch (start us, length us, event | category | flops | bytes accessed | tf_op | source)
XLA Modules:
  0.0 259.1 jit_solution(6370187771592063416)
XLA Ops:
  0.0 2.6 %shard_map.91 = (f32[512,128]{1,0:T(8,128)}, bf16[256,256]{1,0:T(8,128)(2,1)}) custom-call(bf16[128,256]{1,0:T(8,128)(2,1)} %key_ref.3, bf16[128,256]{1,0:T(8,128)(2,1)} %value_ref.3, f32[2,128]{1,0:T(2,128)} %decay_ref.5), custom_call_target="tpu_custom_call" | custom-call | flops 16777216 | bytes 600000 | tf_op jit(solution)/shard_map/pallas_call | solution.py:313
  2.6 20.8 %all-to-all-start = ((f32[512,1,128]{2,1,0:T(1,128)}), f32[512,1,128]{2,1,0:T(1,128)S(1)}, u32[]{:S(2)}, u32[]{:S(2)}) async-start(f32[512,1,128]{2,1,0:T(1,128)} %bitcast.43), calls=%async_computation | async-start | bytes 524288 | tf_op jit(solution)/shard_map/all_to_all | solution.py:297
  23.4 3.4 %collective-permute-start = (bf16[256,256]{1,0:T(8,128)(2,1)}, bf16[256,256]{1,0:T(8,128)(2,1)S(1)}, u32[]{:S(2)}, u32[]{:S(2)}) collective-permute-start(bf16[256,256]{1,0:T(8,128)(2,1)} %get-tuple-element.12), channel_id=1, source_target_pairs={{0,1},{1,2},{2,3},{3,4},{4,5},{5,6},{6,7},{7,8},{8,9},{9,10},{10,1... | collective-permute-start | bytes 393224 | tf_op jit(solution)/shard_map/ppermute | solution.py:322
  27.7 9.7 %all-to-all-done = f32[512,1,128]{2,1,0:T(1,128)S(1)} async-done(((f32[512,1,128]{2,1,0:T(1,128)}), f32[512,1,128]{2,1,0:T(1,128)S(1)}, u32[]{:S(2)}, u32[]{:S(2)}) %all-to-all-start) | async-done | bytes 262176 | tf_op jit(solution)/shard_map/all_to_all | solution.py:297
  38.9 12.1 %all-to-all-start.1 = ((f32[512,1,128]{2,1,0:T(1,128)}), f32[512,1,128]{2,1,0:T(1,128)S(1)}, u32[]{:S(2)}, u32[]{:S(2)}) async-start(f32[512,1,128]{2,1,0:T(1,128)} %bitcast.5), calls=%async_computation.1 | async-start | bytes 524288 | tf_op jit(solution)/shard_map/all_to_all | solution.py:297
  52.2 3.6 %shard_map.93 = (f32[128,2048]{1,0:T(8,128)S(1)}, f32[128,2048]{1,0:T(8,128)S(1)}) custom-call(s32[1]{0:T(128)} %bitcast.8.started_ref, bf16[128,2048]{1,0:T(8,128)(2,1)S(1)} %copy-done, bf16[128,256]{1,0:T(8,128)(2,1)S(1)} %copy-done.1, bf16[128,256]{1,0:T(8,128)(2,1)S(1)} %copy-done.2, bf16[256,256]{1,0:T(8,128)(2,1)S(1)} %collective-permute-done.prev_ref, ...), custom_call_target="tpu_custom_call" | custom-call | flops 536870912 | bytes 3000000 | tf_op jit(solution)/shard_map/pallas_call | solution.py:351
  55.8 9.1 %all-to-all-done.1 = f32[512,1,128]{2,1,0:T(1,128)S(1)} async-done(((f32[512,1,128]{2,1,0:T(1,128)}), f32[512,1,128]{2,1,0:T(1,128)S(1)}, u32[]{:S(2)}, u32[]{:S(2)}) %all-to-all-start.1) | async-done | bytes 262176 | tf_op jit(solution)/shard_map/all_to_all | solution.py:297
  64.9 3.3 %shard_map.94 = (bf16[128,16,128]{2,1,0:T(8,128)(2,1)S(1)}, bf16[384,16,128]{2,1,0:T(8,128)(2,1)}) custom-call(s32[256]{0:T(256)S(1)} %multiply_add_fusion.slot_ref, bf16[128,2048]{1,0:T(8,128)(2,1)S(1)} %copy-done, f32[512,128]{1,0:T(8,128)S(1)} %bitcast.36, f32[2,128]{1,0:T(2,128)S(1)} %copy-done.4, f32[1,2048]{1,0:T(1,128)S(1)} %bitcast.38, ...), custom_call_target="tpu_custom_call" | custom-call | flops 268435456 | bytes 5000000 | tf_op jit(solution)/shard_map/pallas_call | solution.py:359
  68.2 8.1 %all-to-all-start.2 = ((bf16[32,192,128]{2,1,0:T(8,128)(2,1)}), bf16[32,192,128]{2,1,0:T(8,128)(2,1)}, u32[]{:S(2)}, u32[]{:S(2)}) async-start(bf16[32,192,128]{2,1,0:T(8,128)(2,1)} %bitcast.9), calls=%async_computation.2 | async-start | bytes 3145728 | tf_op jit(solution)/shard_map/all_to_all | solution.py:303
  76.4 2.1 shard_map.95
  78.5 3.0 %collective-permute-start.3 = (bf16[176,2048]{1,0:T(8,128)(2,1)}, bf16[176,2048]{1,0:T(8,128)(2,1)S(1)}, u32[]{:S(2)}, u32[]{:S(2)}) collective-permute-start(bf16[176,2048]{1,0:T(8,128)(2,1)} %shard_map.95), channel_id=1, source_target_pairs={{0,8},{4,12},{8,0},{12,4},{16,24},{20,28},{24,16},{28,20},{32,40},... | collective-permute-start | bytes 2162696 | tf_op jit(solution)/shard_map/ppermute | solution.py:293
  81.5 47.3 %collective-permute-done.3.refs_4_ = bf16[176,2048]{1,0:T(8,128)(2,1)S(1)} collective-permute-done((bf16[176,2048]{1,0:T(8,128)(2,1)}, bf16[176,2048]{1,0:T(8,128)(2,1)S(1)}, u32[]{:S(2)}, u32[]{:S(2)}) %collective-permute-start.3) | collective-permute-done | bytes 720928 | tf_op jit(solution)/shard_map/ppermute | solution.py:293
  128.8 3.5 %collective-permute-start.6 = (bf16[176,2048]{1,0:T(8,128)(2,1)S(1)}, bf16[176,2048]{1,0:T(8,128)(2,1)S(1)}, u32[]{:S(2)}, u32[]{:S(2)}) collective-permute-start(bf16[176,2048]{1,0:T(8,128)(2,1)S(1)} %collective-permute-done.3.refs_4_), channel_id=1, source_target_pairs={{0,3},{1,0},{2,1},{3,2},{4,7},{5,4},{6,5},{7,6},{8,11},{9,8},{10,9... | collective-permute-start | bytes 2162696 | tf_op jit(solution)/shard_map/ppermute | solution.py:337
  134.2 2.3 collective-permute-start.4
  136.6 2.1 collective-permute-start.2
  138.7 3.9 %collective-permute-start.5 = (bf16[176,2048]{1,0:T(8,128)(2,1)S(1)}, bf16[176,2048]{1,0:T(8,128)(2,1)S(1)}, u32[]{:S(2)}, u32[]{:S(2)}) collective-permute-start(bf16[176,2048]{1,0:T(8,128)(2,1)S(1)} %collective-permute-done.3.refs_4_), channel_id=1, source_target_pairs={{0,2},{1,3},{2,0},{3,1},{4,6},{5,7},{6,4},{7,5},{8,10},{9,11},{10,... | collective-permute-start | bytes 2162696 | tf_op jit(solution)/shard_map/ppermute | solution.py:337
  142.6 7.0 %collective-permute-done.6.refs_7_ = bf16[176,2048]{1,0:T(8,128)(2,1)S(1)} collective-permute-done((bf16[176,2048]{1,0:T(8,128)(2,1)S(1)}, bf16[176,2048]{1,0:T(8,128)(2,1)S(1)}, u32[]{:S(2)}, u32[]{:S(2)}) %collective-permute-start.6) | collective-permute-done | bytes 720928 | tf_op jit(solution)/shard_map/ppermute | solution.py:337
  149.7 2.1 collective-permute-start.7
  151.8 19.6 %collective-permute-done.4.refs_5_ = bf16[176,2048]{1,0:T(8,128)(2,1)S(1)} collective-permute-done((bf16[176,2048]{1,0:T(8,128)(2,1)S(1)}, bf16[176,2048]{1,0:T(8,128)(2,1)S(1)}, u32[]{:S(2)}, u32[]{:S(2)}) %collective-permute-start.4) | collective-permute-done | bytes 720928 | tf_op jit(solution)/shard_map/ppermute | solution.py:337
  173.3 2.4 collective-permute-start.8
  181.6 8.9 %shard_map.96.weight_ref = bf16[3072,2048]{1,0:T(8,128)(2,1)} custom-call(s32[1]{0:T(128)} %bitcast.11.plane_ref, bf16[352,2048]{1,0:T(8,128)(2,1)} %bitcast.40, bf16[352,2048]{1,0:T(8,128)(2,1)} %refs_1_.1, bf16[352,2048]{1,0:T(8,128)(2,1)} %copy-done.7, bf16[352,2048]{1,0:T(8,128)(2,1)} %copy-done.8, bf16[176,2048]{1,0:T(8,128)(2,1)} %copy-done.9, ...), custom_call_target="tpu_custom_call" | custom-call | bytes 24000000 | tf_op jit(solution)/shard_map/pallas_call | solution.py:369
  190.5 10.8 %shard_map.97 = bf16[384,16,128]{2,1,0:T(8,128)(2,1)} custom-call(bf16[384,16,128]{2,1,0:T(8,128)(2,1)} %bitcast.10.recv_ref, bf16[3072,2048]{1,0:T(8,128)(2,1)} %shard_map.96.weight_ref), custom_call_target="tpu_custom_call" | custom-call | flops 4499999744 | bytes 15000000 | tf_op jit(solution)/shard_map/pallas_call | solution.py:377
  201.3 11.9 %all-to-all-start.3 = ((bf16[32,192,128]{2,1,0:T(8,128)(2,1)}), bf16[32,192,128]{2,1,0:T(8,128)(2,1)S(1)}, u32[]{:S(2)}, u32[]{:S(2)}) async-start(bf16[32,192,128]{2,1,0:T(8,128)(2,1)} %bitcast.42), calls=%async_computation.3 | async-start | bytes 3145728 | tf_op jit(solution)/shard_map/all_to_all | solution.py:303
  213.5 43.7 %all-to-all-done.3 = bf16[32,192,128]{2,1,0:T(8,128)(2,1)S(1)} async-done(((bf16[32,192,128]{2,1,0:T(8,128)(2,1)}), bf16[32,192,128]{2,1,0:T(8,128)(2,1)S(1)}, u32[]{:S(2)}, u32[]{:S(2)}) %all-to-all-start.3) | async-done | bytes 1572896 | tf_op jit(solution)/shard_map/all_to_all | solution.py:303
  (60 shorter events, 15.4 us)
Async XLA Ops:
  0.0 52.1 %copy-start.1 = (bf16[128,256]{1,0:T(8,128)(2,1)S(1)}, bf16[128,256]{1,0:T(8,128)(2,1)}, u32[]{:S(2)}) copy-start(bf16[128,256]{1,0:T(8,128)(2,1)} %key_ref.3) | copy-start | bytes 196612
  0.0 52.1 %copy-start.2 = (bf16[128,256]{1,0:T(8,128)(2,1)S(1)}, bf16[128,256]{1,0:T(8,128)(2,1)}, u32[]{:S(2)}) copy-start(bf16[128,256]{1,0:T(8,128)(2,1)} %value_ref.3) | copy-start | bytes 196612
  0.0 52.2 %copy-start.4 = (f32[2,128]{1,0:T(2,128)S(1)}, f32[2,128]{1,0:T(2,128)}, u32[]{:S(2)}) copy-start(f32[2,128]{1,0:T(2,128)} %decay_ref.5) | copy-start | bytes 3076
  0.0 52.2 %copy-start = (bf16[128,2048]{1,0:T(8,128)(2,1)S(1)}, bf16[128,2048]{1,0:T(8,128)(2,1)}, u32[]{:S(2)}) copy-start(bf16[128,2048]{1,0:T(8,128)(2,1)} %query_ref.3) | copy-start | bytes 1572868
  2.6 34.8 %all-to-all-start = ((f32[512,1,128]{2,1,0:T(1,128)}), f32[512,1,128]{2,1,0:T(1,128)S(1)}, u32[]{:S(2)}, u32[]{:S(2)}) async-start(f32[512,1,128]{2,1,0:T(1,128)} %bitcast.43), calls=%async_computation | async-start | bytes 524288 | tf_op jit(solution)/shard_map/all_to_all | solution.py:297
  23.4 28.7 %collective-permute-start = (bf16[256,256]{1,0:T(8,128)(2,1)}, bf16[256,256]{1,0:T(8,128)(2,1)S(1)}, u32[]{:S(2)}, u32[]{:S(2)}) collective-permute-start(bf16[256,256]{1,0:T(8,128)(2,1)} %get-tuple-element.12), channel_id=1, source_target_pairs={{0,1},{1,2},{2,3},{3,4},{4,5},{5,6},{6,7},{7,8},{8,9},{9,10},{10,1... | collective-permute-start | bytes 393224 | tf_op jit(solution)/shard_map/ppermute | solution.py:322
  37.5 27.5 %copy-start.3 = (f32[2048]{0:T(1024)S(1)}, f32[2048]{0:T(1024)}, u32[]{:S(2)}) copy-start(f32[2048]{0:T(1024)} %param.13) | copy-start | bytes 24580
  38.9 26.0 %all-to-all-start.1 = ((f32[512,1,128]{2,1,0:T(1,128)}), f32[512,1,128]{2,1,0:T(1,128)S(1)}, u32[]{:S(2)}, u32[]{:S(2)}) async-start(f32[512,1,128]{2,1,0:T(1,128)} %bitcast.5), calls=%async_computation.1 | async-start | bytes 524288 | tf_op jit(solution)/shard_map/all_to_all | solution.py:297
  68.2 122.3 %all-to-all-start.2 = ((bf16[32,192,128]{2,1,0:T(8,128)(2,1)}), bf16[32,192,128]{2,1,0:T(8,128)(2,1)}, u32[]{:S(2)}, u32[]{:S(2)}) async-start(bf16[32,192,128]{2,1,0:T(8,128)(2,1)} %bitcast.9), calls=%async_computation.2 | async-start | bytes 3145728 | tf_op jit(solution)/shard_map/all_to_all | solution.py:303
  76.3 56.0 %copy-start.5 = (bf16[2048,352]{0,1:T(8,128)(2,1)S(1)}, bf16[2048,352]{0,1:T(8,128)(2,1)}, u32[]{:S(2)}) copy-start(bf16[2048,352]{0,1:T(8,128)(2,1)} %param.16) | copy-start | bytes 4325380
  76.4 60.2 %copy-start.6 = (bf16[352,2048]{1,0:T(8,128)(2,1)S(1)}, bf16[352,2048]{1,0:T(8,128)(2,1)}, u32[]{:S(2)}) copy-start(bf16[352,2048]{1,0:T(8,128)(2,1)} %refs_1_.1) | copy-start | bytes 4325380
  78.5 50.3 %collective-permute-start.3 = (bf16[176,2048]{1,0:T(8,128)(2,1)}, bf16[176,2048]{1,0:T(8,128)(2,1)S(1)}, u32[]{:S(2)}, u32[]{:S(2)}) collective-permute-start(bf16[176,2048]{1,0:T(8,128)(2,1)} %shard_map.95), channel_id=1, source_target_pairs={{0,8},{4,12},{8,0},{12,4},{16,24},{20,28},{24,16},{28,20},{32,40},... | collective-permute-start | bytes 2162696 | tf_op jit(solution)/shard_map/ppermute | solution.py:293
  128.8 52.8 %copy-start.9 = (bf16[176,2048]{1,0:T(8,128)(2,1)}, bf16[176,2048]{1,0:T(8,128)(2,1)S(1)}, u32[]{:S(2)}) copy-start(bf16[176,2048]{1,0:T(8,128)(2,1)S(1)} %collective-permute-done.3.refs_4_) | copy-start | bytes 2162692
  128.8 20.9 %collective-permute-start.6 = (bf16[176,2048]{1,0:T(8,128)(2,1)S(1)}, bf16[176,2048]{1,0:T(8,128)(2,1)S(1)}, u32[]{:S(2)}, u32[]{:S(2)}) collective-permute-start(bf16[176,2048]{1,0:T(8,128)(2,1)S(1)} %collective-permute-done.3.refs_4_), channel_id=1, source_target_pairs={{0,3},{1,0},{2,1},{3,2},{4,7},{5,4},{6,5},{7,6},{8,11},{9,8},{10,9... | collective-permute-start | bytes 2162696 | tf_op jit(solution)/shard_map/ppermute | solution.py:337
  132.3 45.3 %collective-permute-start.1 = (bf16[352,2048]{1,0:T(8,128)(2,1)S(1)}, bf16[352,2048]{1,0:T(8,128)(2,1)S(1)}, u32[]{:S(2)}, u32[]{:S(2)}) collective-permute-start(bf16[352,2048]{1,0:T(8,128)(2,1)S(1)} %bitcast.41), channel_id=1, source_target_pairs={{0,4},{4,0},{8,12},{12,8},{16,20},{20,16},{24,28},{28,24},{32,36},... | collective-permute-start | bytes 4325384 | tf_op jit(solution)/shard_map/ppermute | solution.py:293
  134.2 37.1 %collective-permute-start.4 = (bf16[176,2048]{1,0:T(8,128)(2,1)S(1)}, bf16[176,2048]{1,0:T(8,128)(2,1)S(1)}, u32[]{:S(2)}, u32[]{:S(2)}) collective-permute-start(bf16[176,2048]{1,0:T(8,128)(2,1)S(1)} %collective-permute-done.3.refs_4_), channel_id=1, source_target_pairs={{0,1},{1,2},{2,3},{3,0},{4,5},{5,6},{6,7},{7,4},{8,9},{9,10},{10,1... | collective-permute-start | bytes 2162696 | tf_op jit(solution)/shard_map/ppermute | solution.py:337
  136.6 41.1 %collective-permute-start.2 = (bf16[352,2048]{1,0:T(8,128)(2,1)S(1)}, bf16[352,2048]{1,0:T(8,128)(2,1)S(1)}, u32[]{:S(2)}, u32[]{:S(2)}) collective-permute-start(bf16[352,2048]{1,0:T(8,128)(2,1)S(1)} %copy-done.6), channel_id=1, source_target_pairs={{0,4},{4,0},{8,12},{12,8},{16,20},{20,16},{24,28},{28,24},{32,36},... | collective-permute-start | bytes 4325384 | tf_op jit(solution)/shard_map/ppermute | solution.py:293
  138.7 34.5 %collective-permute-start.5 = (bf16[176,2048]{1,0:T(8,128)(2,1)S(1)}, bf16[176,2048]{1,0:T(8,128)(2,1)S(1)}, u32[]{:S(2)}, u32[]{:S(2)}) collective-permute-start(bf16[176,2048]{1,0:T(8,128)(2,1)S(1)} %collective-permute-done.3.refs_4_), channel_id=1, source_target_pairs={{0,2},{1,3},{2,0},{3,1},{4,6},{5,7},{6,4},{7,5},{8,10},{9,11},{10,... | collective-permute-start | bytes 2162696 | tf_op jit(solution)/shard_map/ppermute | solution.py:337
  149.7 30.2 %copy-start.10 = (bf16[176,2048]{1,0:T(8,128)(2,1)}, bf16[176,2048]{1,0:T(8,128)(2,1)S(1)}, u32[]{:S(2)}) copy-start(bf16[176,2048]{1,0:T(8,128)(2,1)S(1)} %collective-permute-done.6.refs_7_) | copy-start | bytes 2162692
  149.7 26.0 %collective-permute-start.7 = (bf16[176,2048]{1,0:T(8,128)(2,1)S(1)}, bf16[176,2048]{1,0:T(8,128)(2,1)S(1)}, u32[]{:S(2)}, u32[]{:S(2)}) collective-permute-start(bf16[176,2048]{1,0:T(8,128)(2,1)S(1)} %collective-permute-done.3.refs_4_), channel_id=1, source_target_pairs={{0,4},{4,0},{8,12},{12,8},{16,20},{20,16},{24,28},{28,24},{32,36},... | collective-permute-start | bytes 2162696 | tf_op jit(solution)/shard_map/ppermute | solution.py:293
  171.3 7.4 %collective-permute-start.10 = (bf16[176,2048]{1,0:T(8,128)(2,1)S(1)}, bf16[176,2048]{1,0:T(8,128)(2,1)S(1)}, u32[]{:S(2)}, u32[]{:S(2)}) collective-permute-start(bf16[176,2048]{1,0:T(8,128)(2,1)S(1)} %collective-permute-done.6.refs_7_), channel_id=1, source_target_pairs={{0,4},{4,0},{8,12},{12,8},{16,20},{20,16},{24,28},{28,24},{32,36},... | collective-permute-start | bytes 2162696 | tf_op jit(solution)/shard_map/ppermute | solution.py:293
  173.3 6.6 %collective-permute-start.8 = (bf16[176,2048]{1,0:T(8,128)(2,1)S(1)}, bf16[176,2048]{1,0:T(8,128)(2,1)S(1)}, u32[]{:S(2)}, u32[]{:S(2)}) collective-permute-start(bf16[176,2048]{1,0:T(8,128)(2,1)S(1)} %collective-permute-done.4.refs_5_), channel_id=1, source_target_pairs={{0,4},{4,0},{8,12},{12,8},{16,20},{20,16},{24,28},{28,24},{32,36},... | collective-permute-start | bytes 2162696 | tf_op jit(solution)/shard_map/ppermute | solution.py:293
  175.7 5.9 %collective-permute-start.9 = (bf16[176,2048]{1,0:T(8,128)(2,1)S(1)}, bf16[176,2048]{1,0:T(8,128)(2,1)}, u32[]{:S(2)}, u32[]{:S(2)}) collective-permute-start(bf16[176,2048]{1,0:T(8,128)(2,1)S(1)} %collective-permute-done.5.refs_6_), channel_id=1, source_target_pairs={{0,4},{4,0},{8,12},{12,8},{16,20},{20,16},{24,28},{28,24},{32,36},... | collective-permute-start | bytes 2162696 | tf_op jit(solution)/shard_map/ppermute | solution.py:293
  201.3 55.9 %all-to-all-start.3 = ((bf16[32,192,128]{2,1,0:T(8,128)(2,1)}), bf16[32,192,128]{2,1,0:T(8,128)(2,1)S(1)}, u32[]{:S(2)}, u32[]{:S(2)}) async-start(bf16[32,192,128]{2,1,0:T(8,128)(2,1)} %bitcast.42), calls=%async_computation.3 | async-start | bytes 3145728 | tf_op jit(solution)/shard_map/all_to_all | solution.py:303
  (8 other events, 35.3 us)

commit v4 on v3

--- a/solution.py
+++ b/solution.py
@@ -154,7 +154,7 @@
         send_ref[slot_ref[2 * t + 1]] = row
         return carry
 
-    lax.fori_loop(0, TOK, place, 0, unroll=16)
+    lax.fori_loop(0, TOK, place, 0, unroll=32)
 
 
 def pick_kernel(plane_ref, up_ref, down_ref, piece_ref, sem):
@@ -220,7 +220,7 @@
 
     for n in range(SLOTS // CHUNK):
         arrivals[n].wait()
-        lax.fori_loop(n * CHUNK, (n + 1) * CHUNK, unpack, 0, unroll=16)
+        lax.fori_loop(n * CHUNK, (n + 1) * CHUNK, unpack, 0, unroll=CHUNK)
     for j in range(HEADS):
         x_ref[:, j * HEAD : (j + 1) * HEAD] = rows_ref[
             pl.ds(j, SLOTS, stride=PITCH), :
@@ -248,7 +248,7 @@
 
     leaving = []
     for n in range(SLOTS // CHUNK):
-        lax.fori_loop(n * CHUNK, (n + 1) * CHUNK, pack, 0, unroll=16)
+        lax.fori_loop(n * CHUNK, (n + 1) * CHUNK, pack, 0, unroll=CHUNK)
         some = pl.ds(n * CHUNK, CHUNK)
         leaving.append(pltpu.make_async_copy(tiles_ref.at[some], out_ref.at[some], sems.at[n]))
         leaving[n].start()
@@ -263,7 +263,7 @@
         rows_ref[pl.ds(t * PITCH, HEADS), :] = attn_ref[t].astype(F32) + moe
         return carry
 
-    lax.fori_loop(0, TOK, one, 0, unroll=8)
+    lax.fori_loop(0, TOK, one, 0, unroll=32)
     for j in range(HEADS):
         out_ref[:, j * HEAD : (j + 1) * HEAD] = rows_ref[
             pl.ds(j, TOK, stride=PITCH), :
@@ -371,7 +371,7 @@
         [((2 * PADDED, WIDTH), BF16)],
         [SMEM] + [FAR] * 12,
         [pltpu.SemaphoreType.DMA((12,))],
-        room=62,
+        room=44,
         moved=24_000_000,
     )(plane, up, w_down, up_c, down_c, *pieces, *onward)
     computed = call(

time: 260 us -> 257 us (0.988)
  the two profiles are of different devices: /device:TPU:48 before, /device:TPU:32 now
where the time goes in v4:
time: 257 us; the launch traced here: 256 us
  waiting for transfers between devices  133 us (52%)
  starting transfers between devices  86.9 us (34%)
  Pallas kernels  33.7 us (13%)
    ppermute x7, waiting for transfers between devices, swapped(): return lax.ppermute(x, 'wide', [(i, i ^ bit) for i in range(peers)])  49.6 us
    all_to_all x2, waiting for transfers between devices, routed(): lax.all_to_all(flat, 'wide', split_axis=0, concat_axis=0, tiled=True, axi...  43.3 us
    all_to_all x2, starting transfers between devices, exchanged(): return lax.all_to_all(x, axis, split_axis=0, concat_axis=0, tiled=True)  34.4 us
    all_to_all x2, starting transfers between devices, routed(): lax.all_to_all(flat, 'wide', split_axis=0, concat_axis=0, tiled=True, axi...  24 us
    ppermute x3, waiting for transfers between devices, per_device(): pieces.append(lax.ppermute(pieces[0], 'narrow', around))  24 us
    all_to_all x2, waiting for transfers between devices, exchanged(): return lax.all_to_all(x, axis, split_axis=0, concat_axis=0, tiled=True)  16 us
    ppermute x7, starting transfers between devices, swapped(): return lax.ppermute(x, 'wide', [(i, i ^ bit) for i in range(peers)])  15.4 us
    pallas_call x1, Pallas kernels, per_device(): call(expert_kernel, [((SLOTS, HEADS, HEAD), BF16)], [FAR] * 2, [pltpu.VME...  10.7 us
  transfers between devices with their start and end apart: 15, of which 8 were waited for; matrix products, arithmetic and copies ran while one was open for 1% of the time, Pallas kernels for 6%

profile of v4, /device:TPU:32, one launch (start us, length us, event | category | flops | bytes accessed | tf_op | source)
XLA Modules:
  0.0 256.0 jit_solution(6008138148252942120)
XLA Ops:
  0.0 2.6 %shard_map.91 = (f32[512,128]{1,0:T(8,128)}, bf16[256,256]{1,0:T(8,128)(2,1)}) custom-call(bf16[128,256]{1,0:T(8,128)(2,1)} %key_ref.3, bf16[128,256]{1,0:T(8,128)(2,1)} %value_ref.3, f32[2,128]{1,0:T(2,128)} %decay_ref.5), custom_call_target="tpu_custom_call" | custom-call | flops 16777216 | bytes 600000 | tf_op jit(solution)/shard_map/pallas_call | solution.py:313
  2.6 20.9 %all-to-all-start = ((f32[512,1,128]{2,1,0:T(1,128)}), f32[512,1,128]{2,1,0:T(1,128)S(1)}, u32[]{:S(2)}, u32[]{:S(2)}) async-start(f32[512,1,128]{2,1,0:T(1,128)} %bitcast.43), calls=%async_computation | async-start | bytes 524288 | tf_op jit(solution)/shard_map/all_to_all | solution.py:297
  23.5 3.4 %collective-permute-start = (bf16[256,256]{1,0:T(8,128)(2,1)}, bf16[256,256]{1,0:T(8,128)(2,1)S(1)}, u32[]{:S(2)}, u32[]{:S(2)}) collective-permute-start(bf16[256,256]{1,0:T(8,128)(2,1)} %get-tuple-element.12), channel_id=1, source_target_pairs={{0,1},{1,2},{2,3},{3,4},{4,5},{5,6},{6,7},{7,8},{8,9},{9,10},{10,1... | collective-permute-start | bytes 393224 | tf_op jit(solution)/shard_map/ppermute | solution.py:322
  27.8 8.3 %all-to-all-done = f32[512,1,128]{2,1,0:T(1,128)S(1)} async-done(((f32[512,1,128]{2,1,0:T(1,128)}), f32[512,1,128]{2,1,0:T(1,128)S(1)}, u32[]{:S(2)}, u32[]{:S(2)}) %all-to-all-start) | async-done | bytes 262176 | tf_op jit(solution)/shard_map/all_to_all | solution.py:297
  37.6 13.5 %all-to-all-start.1 = ((f32[512,1,128]{2,1,0:T(1,128)}), f32[512,1,128]{2,1,0:T(1,128)S(1)}, u32[]{:S(2)}, u32[]{:S(2)}) async-start(f32[512,1,128]{2,1,0:T(1,128)} %bitcast.5), calls=%async_computation.1 | async-start | bytes 524288 | tf_op jit(solution)/shard_map/all_to_all | solution.py:297
  52.3 3.6 %shard_map.93 = (f32[128,2048]{1,0:T(8,128)S(1)}, f32[128,2048]{1,0:T(8,128)S(1)}) custom-call(s32[1]{0:T(128)} %bitcast.8.started_ref, bf16[128,2048]{1,0:T(8,128)(2,1)S(1)} %copy-done.2, bf16[128,256]{1,0:T(8,128)(2,1)S(1)} %copy-done.3, bf16[128,256]{1,0:T(8,128)(2,1)S(1)} %copy-done.4, bf16[256,256]{1,0:T(8,128)(2,1)S(1)} %collective-permute-done.prev_ref, ...), custom_call_target="tpu_custom_call" | custom-call | flops 536870912 | bytes 3000000 | tf_op jit(solution)/shard_map/pallas_call | solution.py:351
  55.9 7.7 %all-to-all-done.1 = f32[512,1,128]{2,1,0:T(1,128)S(1)} async-done(((f32[512,1,128]{2,1,0:T(1,128)}), f32[512,1,128]{2,1,0:T(1,128)S(1)}, u32[]{:S(2)}, u32[]{:S(2)}) %all-to-all-start.1) | async-done | bytes 262176 | tf_op jit(solution)/shard_map/all_to_all | solution.py:297
  63.6 3.3 %shard_map.94 = (bf16[128,16,128]{2,1,0:T(8,128)(2,1)S(1)}, bf16[384,16,128]{2,1,0:T(8,128)(2,1)}) custom-call(s32[256]{0:T(256)S(1)} %multiply_add_fusion.slot_ref, bf16[128,2048]{1,0:T(8,128)(2,1)S(1)} %copy-done.2, f32[512,128]{1,0:T(8,128)S(1)} %bitcast.39, f32[2,128]{1,0:T(2,128)S(1)} %copy-done.6, f32[1,2048]{1,0:T(1,128)S(1)} %bitcast.41, ...), custom_call_target="tpu_custom_call" | custom-call | flops 268435456 | bytes 5000000 | tf_op jit(solution)/shard_map/pallas_call | solution.py:359
  66.9 9.6 %all-to-all-start.2 = ((bf16[32,192,128]{2,1,0:T(8,128)(2,1)}), bf16[32,192,128]{2,1,0:T(8,128)(2,1)}, u32[]{:S(2)}, u32[]{:S(2)}) async-start(bf16[32,192,128]{2,1,0:T(8,128)(2,1)} %bitcast.9), calls=%async_computation.2 | async-start | bytes 3145728 | tf_op jit(solution)/shard_map/all_to_all | solution.py:303
  76.5 2.2 shard_map.95
  78.7 3.0 %collective-permute-start.3 = (bf16[176,2048]{1,0:T(8,128)(2,1)}, bf16[176,2048]{1,0:T(8,128)(2,1)S(1)}, u32[]{:S(2)}, u32[]{:S(2)}) collective-permute-start(bf16[176,2048]{1,0:T(8,128)(2,1)} %shard_map.95), channel_id=1, source_target_pairs={{0,8},{4,12},{8,0},{12,4},{16,24},{20,28},{24,16},{28,20},{32,40},... | collective-permute-start | bytes 2162696 | tf_op jit(solution)/shard_map/ppermute | solution.py:293
  81.7 47.9 %collective-permute-done.3.refs_4_ = bf16[176,2048]{1,0:T(8,128)(2,1)S(1)} collective-permute-done((bf16[176,2048]{1,0:T(8,128)(2,1)}, bf16[176,2048]{1,0:T(8,128)(2,1)S(1)}, u32[]{:S(2)}, u32[]{:S(2)}) %collective-permute-start.3) | collective-permute-done | bytes 720928 | tf_op jit(solution)/shard_map/ppermute | solution.py:293
  129.5 2.7 %collective-permute-start.6 = (bf16[176,2048]{1,0:T(8,128)(2,1)S(1)}, bf16[176,2048]{1,0:T(8,128)(2,1)S(1)}, u32[]{:S(2)}, u32[]{:S(2)}) collective-permute-start(bf16[176,2048]{1,0:T(8,128)(2,1)S(1)} %collective-permute-done.3.refs_4_), channel_id=1, source_target_pairs={{0,3},{1,0},{2,1},{3,2},{4,7},{5,4},{6,5},{7,6},{8,11},{9,8},{10,9... | collective-permute-start | bytes 2162696 | tf_op jit(solution)/shard_map/ppermute | solution.py:337
  134.2 3.1 %collective-permute-start.4 = (bf16[176,2048]{1,0:T(8,128)(2,1)S(1)}, bf16[176,2048]{1,0:T(8,128)(2,1)S(1)}, u32[]{:S(2)}, u32[]{:S(2)}) collective-permute-start(bf16[176,2048]{1,0:T(8,128)(2,1)S(1)} %collective-permute-done.3.refs_4_), channel_id=1, source_target_pairs={{0,1},{1,2},{2,3},{3,0},{4,5},{5,6},{6,7},{7,4},{8,9},{9,10},{10,1... | collective-permute-start | bytes 2162696 | tf_op jit(solution)/shard_map/ppermute | solution.py:337
  137.3 2.1 collective-permute-start.2
  139.4 3.8 %collective-permute-start.5 = (bf16[176,2048]{1,0:T(8,128)(2,1)S(1)}, bf16[176,2048]{1,0:T(8,128)(2,1)S(1)}, u32[]{:S(2)}, u32[]{:S(2)}) collective-permute-start(bf16[176,2048]{1,0:T(8,128)(2,1)S(1)} %collective-permute-done.3.refs_4_), channel_id=1, source_target_pairs={{0,2},{1,3},{2,0},{3,1},{4,6},{5,7},{6,4},{7,5},{8,10},{9,11},{10,... | collective-permute-start | bytes 2162696 | tf_op jit(solution)/shard_map/ppermute | solution.py:337
  143.3 7.1 %collective-permute-done.6.refs_7_ = bf16[176,2048]{1,0:T(8,128)(2,1)S(1)} collective-permute-done((bf16[176,2048]{1,0:T(8,128)(2,1)S(1)}, bf16[176,2048]{1,0:T(8,128)(2,1)S(1)}, u32[]{:S(2)}, u32[]{:S(2)}) %collective-permute-start.6) | collective-permute-done | bytes 720928 | tf_op jit(solution)/shard_map/ppermute | solution.py:337
  152.5 3.8 %collective-permute-done.4.refs_5_ = bf16[176,2048]{1,0:T(8,128)(2,1)S(1)} collective-permute-done((bf16[176,2048]{1,0:T(8,128)(2,1)S(1)}, bf16[176,2048]{1,0:T(8,128)(2,1)S(1)}, u32[]{:S(2)}, u32[]{:S(2)}) %collective-permute-start.4) | collective-permute-done | bytes 720928 | tf_op jit(solution)/shard_map/ppermute | solution.py:337
  158.2 13.0 %collective-permute-done.5.refs_6_ = bf16[176,2048]{1,0:T(8,128)(2,1)S(1)} collective-permute-done((bf16[176,2048]{1,0:T(8,128)(2,1)S(1)}, bf16[176,2048]{1,0:T(8,128)(2,1)S(1)}, u32[]{:S(2)}, u32[]{:S(2)}) %collective-permute-start.5) | collective-permute-done | bytes 720928 | tf_op jit(solution)/shard_map/ppermute | solution.py:337
  173.2 2.4 collective-permute-start.9
  177.4 8.0 %shard_map.96.weight_ref = bf16[3072,2048]{1,0:T(8,128)(2,1)} custom-call(s32[1]{0:T(128)} %bitcast.11.plane_ref, bf16[352,2048]{1,0:T(8,128)(2,1)S(1)} %bitcast.38, bf16[352,2048]{1,0:T(8,128)(2,1)S(1)} %copy-done.1, bf16[352,2048]{1,0:T(8,128)(2,1)S(1)} %collective-permute-done.1.refs_2_, bf16[352,2048]{1,0:T(8,128)(2,1)} %copy-done.7, ...), custom_call_target="tpu_custom_call" | custom-call | bytes 24000000 | tf_op jit(solution)/shard_map/pallas_call | solution.py:369
  185.5 10.7 %shard_map.97 = bf16[384,16,128]{2,1,0:T(8,128)(2,1)} custom-call(bf16[384,16,128]{2,1,0:T(8,128)(2,1)} %bitcast.10.recv_ref, bf16[3072,2048]{1,0:T(8,128)(2,1)} %shard_map.96.weight_ref), custom_call_target="tpu_custom_call" | custom-call | flops 4499999744 | bytes 15000000 | tf_op jit(solution)/shard_map/pallas_call | solution.py:377
  196.2 14.4 %all-to-all-start.3 = ((bf16[32,192,128]{2,1,0:T(8,128)(2,1)}), bf16[32,192,128]{2,1,0:T(8,128)(2,1)S(1)}, u32[]{:S(2)}, u32[]{:S(2)}) async-start(bf16[32,192,128]{2,1,0:T(8,128)(2,1)} %bitcast.42), calls=%async_computation.3 | async-start | bytes 3145728 | tf_op jit(solution)/shard_map/all_to_all | solution.py:303
  210.9 43.3 %all-to-all-done.3 = bf16[32,192,128]{2,1,0:T(8,128)(2,1)S(1)} async-done(((bf16[32,192,128]{2,1,0:T(8,128)(2,1)}), bf16[32,192,128]{2,1,0:T(8,128)(2,1)S(1)}, u32[]{:S(2)}, u32[]{:S(2)}) %all-to-all-start.3) | async-done | bytes 1572896 | tf_op jit(solution)/shard_map/all_to_all | solution.py:303
  (44 shorter events, 15.2 us)
Async XLA Ops:
  0.0 52.2 %copy-start.3 = (bf16[128,256]{1,0:T(8,128)(2,1)S(1)}, bf16[128,256]{1,0:T(8,128)(2,1)}, u32[]{:S(2)}) copy-start(bf16[128,256]{1,0:T(8,128)(2,1)} %key_ref.3) | copy-start | bytes 196612
  0.0 52.2 %copy-start.4 = (bf16[128,256]{1,0:T(8,128)(2,1)S(1)}, bf16[128,256]{1,0:T(8,128)(2,1)}, u32[]{:S(2)}) copy-start(bf16[128,256]{1,0:T(8,128)(2,1)} %value_ref.3) | copy-start | bytes 196612
  0.0 52.2 %copy-start.6 = (f32[2,128]{1,0:T(2,128)S(1)}, f32[2,128]{1,0:T(2,128)}, u32[]{:S(2)}) copy-start(f32[2,128]{1,0:T(2,128)} %decay_ref.5) | copy-start | bytes 3076
  0.0 52.2 %copy-start.2 = (bf16[128,2048]{1,0:T(8,128)(2,1)S(1)}, bf16[128,2048]{1,0:T(8,128)(2,1)}, u32[]{:S(2)}) copy-start(bf16[128,2048]{1,0:T(8,128)(2,1)} %query_ref.3) | copy-start | bytes 1572868
  2.6 33.5 %all-to-all-start = ((f32[512,1,128]{2,1,0:T(1,128)}), f32[512,1,128]{2,1,0:T(1,128)S(1)}, u32[]{:S(2)}, u32[]{:S(2)}) async-start(f32[512,1,128]{2,1,0:T(1,128)} %bitcast.43), calls=%async_computation | async-start | bytes 524288 | tf_op jit(solution)/shard_map/all_to_all | solution.py:297
  23.5 28.7 %collective-permute-start = (bf16[256,256]{1,0:T(8,128)(2,1)}, bf16[256,256]{1,0:T(8,128)(2,1)S(1)}, u32[]{:S(2)}, u32[]{:S(2)}) collective-permute-start(bf16[256,256]{1,0:T(8,128)(2,1)} %get-tuple-element.12), channel_id=1, source_target_pairs={{0,1},{1,2},{2,3},{3,4},{4,5},{5,6},{6,7},{7,8},{8,9},{9,10},{10,1... | collective-permute-start | bytes 393224 | tf_op jit(solution)/shard_map/ppermute | solution.py:322
  36.1 27.5 %copy-start.5 = (f32[2048]{0:T(1024)S(1)}, f32[2048]{0:T(1024)}, u32[]{:S(2)}) copy-start(f32[2048]{0:T(1024)} %param.13) | copy-start | bytes 24580
  37.6 26.0 %all-to-all-start.1 = ((f32[512,1,128]{2,1,0:T(1,128)}), f32[512,1,128]{2,1,0:T(1,128)S(1)}, u32[]{:S(2)}, u32[]{:S(2)}) async-start(f32[512,1,128]{2,1,0:T(1,128)} %bitcast.5), calls=%async_computation.1 | async-start | bytes 524288 | tf_op jit(solution)/shard_map/all_to_all | solution.py:297
  66.9 118.6 %all-to-all-start.2 = ((bf16[32,192,128]{2,1,0:T(8,128)(2,1)}), bf16[32,192,128]{2,1,0:T(8,128)(2,1)}, u32[]{:S(2)}, u32[]{:S(2)}) async-start(bf16[32,192,128]{2,1,0:T(8,128)(2,1)} %bitcast.9), calls=%async_computation.2 | async-start | bytes 3145728 | tf_op jit(solution)/shard_map/all_to_all | solution.py:303
  76.5 55.8 %copy-start = (bf16[2048,352]{0,1:T(8,128)(2,1)S(1)}, bf16[2048,352]{0,1:T(8,128)(2,1)}, u32[]{:S(2)}) copy-start(bf16[2048,352]{0,1:T(8,128)(2,1)} %param.16) | copy-start | bytes 4325380
  76.5 60.8 %copy-start.1 = (bf16[352,2048]{1,0:T(8,128)(2,1)S(1)}, bf16[352,2048]{1,0:T(8,128)(2,1)}, u32[]{:S(2)}) copy-start(bf16[352,2048]{1,0:T(8,128)(2,1)} %refs_1_.1) | copy-start | bytes 4325380
  78.7 50.9 %collective-permute-start.3 = (bf16[176,2048]{1,0:T(8,128)(2,1)}, bf16[176,2048]{1,0:T(8,128)(2,1)S(1)}, u32[]{:S(2)}, u32[]{:S(2)}) collective-permute-start(bf16[176,2048]{1,0:T(8,128)(2,1)} %shard_map.95), channel_id=1, source_target_pairs={{0,8},{4,12},{8,0},{12,4},{16,24},{20,28},{24,16},{28,20},{32,40},... | collective-permute-start | bytes 2162696 | tf_op jit(solution)/shard_map/ppermute | solution.py:293
  129.5 20.9 %collective-permute-start.6 = (bf16[176,2048]{1,0:T(8,128)(2,1)S(1)}, bf16[176,2048]{1,0:T(8,128)(2,1)S(1)}, u32[]{:S(2)}, u32[]{:S(2)}) collective-permute-start(bf16[176,2048]{1,0:T(8,128)(2,1)S(1)} %collective-permute-done.3.refs_4_), channel_id=1, source_target_pairs={{0,3},{1,0},{2,1},{3,2},{4,7},{5,4},{6,5},{7,6},{8,11},{9,8},{10,9... | collective-permute-start | bytes 2162696 | tf_op jit(solution)/shard_map/ppermute | solution.py:337
  132.3 43.4 %collective-permute-start.1 = (bf16[352,2048]{1,0:T(8,128)(2,1)S(1)}, bf16[352,2048]{1,0:T(8,128)(2,1)S(1)}, u32[]{:S(2)}, u32[]{:S(2)}) collective-permute-start(bf16[352,2048]{1,0:T(8,128)(2,1)S(1)} %bitcast.37), channel_id=1, source_target_pairs={{0,4},{4,0},{8,12},{12,8},{16,20},{20,16},{24,28},{28,24},{32,36},... | collective-permute-start | bytes 4325384 | tf_op jit(solution)/shard_map/ppermute | solution.py:293
  134.2 22.1 %collective-permute-start.4 = (bf16[176,2048]{1,0:T(8,128)(2,1)S(1)}, bf16[176,2048]{1,0:T(8,128)(2,1)S(1)}, u32[]{:S(2)}, u32[]{:S(2)}) collective-permute-start(bf16[176,2048]{1,0:T(8,128)(2,1)S(1)} %collective-permute-done.3.refs_4_), channel_id=1, source_target_pairs={{0,1},{1,2},{2,3},{3,0},{4,5},{5,6},{6,7},{7,4},{8,9},{9,10},{10,1... | collective-permute-start | bytes 2162696 | tf_op jit(solution)/shard_map/ppermute | solution.py:337
  137.3 38.3 %collective-permute-start.2 = (bf16[352,2048]{1,0:T(8,128)(2,1)S(1)}, bf16[352,2048]{1,0:T(8,128)(2,1)S(1)}, u32[]{:S(2)}, u32[]{:S(2)}) collective-permute-start(bf16[352,2048]{1,0:T(8,128)(2,1)S(1)} %copy-done.1), channel_id=1, source_target_pairs={{0,4},{4,0},{8,12},{12,8},{16,20},{20,16},{24,28},{28,24},{32,36},... | collective-permute-start | bytes 4325384 | tf_op jit(solution)/shard_map/ppermute | solution.py:293
  139.4 31.8 %collective-permute-start.5 = (bf16[176,2048]{1,0:T(8,128)(2,1)S(1)}, bf16[176,2048]{1,0:T(8,128)(2,1)S(1)}, u32[]{:S(2)}, u32[]{:S(2)}) collective-permute-start(bf16[176,2048]{1,0:T(8,128)(2,1)S(1)} %collective-permute-done.3.refs_4_), channel_id=1, source_target_pairs={{0,2},{1,3},{2,0},{3,1},{4,6},{5,7},{6,4},{7,5},{8,10},{9,11},{10,... | collective-permute-start | bytes 2162696 | tf_op jit(solution)/shard_map/ppermute | solution.py:337
  150.4 22.8 %collective-permute-start.7 = (bf16[176,2048]{1,0:T(8,128)(2,1)S(1)}, bf16[176,2048]{1,0:T(8,128)(2,1)S(1)}, u32[]{:S(2)}, u32[]{:S(2)}) collective-permute-start(bf16[176,2048]{1,0:T(8,128)(2,1)S(1)} %collective-permute-done.3.refs_4_), channel_id=1, source_target_pairs={{0,4},{4,0},{8,12},{12,8},{16,20},{20,16},{24,28},{28,24},{32,36},... | collective-permute-start | bytes 2162696 | tf_op jit(solution)/shard_map/ppermute | solution.py:293
  156.3 19.3 %collective-permute-start.10 = (bf16[176,2048]{1,0:T(8,128)(2,1)S(1)}, bf16[176,2048]{1,0:T(8,128)(2,1)S(1)}, u32[]{:S(2)}, u32[]{:S(2)}) collective-permute-start(bf16[176,2048]{1,0:T(8,128)(2,1)S(1)} %collective-permute-done.6.refs_7_), channel_id=1, source_target_pairs={{0,4},{4,0},{8,12},{12,8},{16,20},{20,16},{24,28},{28,24},{32,36},... | collective-permute-start | bytes 2162696 | tf_op jit(solution)/shard_map/ppermute | solution.py:293
  171.3 4.4 %collective-permute-start.8 = (bf16[176,2048]{1,0:T(8,128)(2,1)S(1)}, bf16[176,2048]{1,0:T(8,128)(2,1)S(1)}, u32[]{:S(2)}, u32[]{:S(2)}) collective-permute-start(bf16[176,2048]{1,0:T(8,128)(2,1)S(1)} %collective-permute-done.4.refs_5_), channel_id=1, source_target_pairs={{0,4},{4,0},{8,12},{12,8},{16,20},{20,16},{24,28},{28,24},{32,36},... | collective-permute-start | bytes 2162696 | tf_op jit(solution)/shard_map/ppermute | solution.py:293
  173.2 4.2 %collective-permute-start.9 = (bf16[176,2048]{1,0:T(8,128)(2,1)S(1)}, bf16[176,2048]{1,0:T(8,128)(2,1)S(1)}, u32[]{:S(2)}, u32[]{:S(2)}) collective-permute-start(bf16[176,2048]{1,0:T(8,128)(2,1)S(1)} %collective-permute-done.5.refs_6_), channel_id=1, source_target_pairs={{0,4},{4,0},{8,12},{12,8},{16,20},{20,16},{24,28},{28,24},{32,36},... | collective-permute-start | bytes 2162696 | tf_op jit(solution)/shard_map/ppermute | solution.py:293
  175.6 1.8 copy-start.7
  196.2 14.5 %copy-start.8 = (f32[128,2]{0,1:T(2,128)S(1)}, f32[128,2]{0,1:T(2,128)}, u32[]{:S(2)}) copy-start(f32[128,2]{0,1:T(2,128)} %param.15) | copy-start | bytes 3076
  196.2 58.0 %all-to-all-start.3 = ((bf16[32,192,128]{2,1,0:T(8,128)(2,1)}), bf16[32,192,128]{2,1,0:T(8,128)(2,1)S(1)}, u32[]{:S(2)}, u32[]{:S(2)}) async-start(bf16[32,192,128]{2,1,0:T(8,128)(2,1)} %bitcast.42), calls=%async_computation.3 | async-start | bytes 3145728 | tf_op jit(solution)/shard_map/all_to_all | solution.py:303
